TPU v7x, 128 devices: a whole 4x4x4 slice. The times are simulated.
128 devices in a mesh: seq: 32 (over z, x, core), dp: 4 (over y).
Axes of the slice: x: 4, y: 4, z: 4, core: 2. Of those that a mesh axis runs over, the one named last changes fastest.
Arguments:
- queries: bfloat16 [4, 8192, 1536], P('dp', 'seq'), may hold values from -6 to 6
- key_vectors: bfloat16 [4, 8192, 1536], P('dp', 'seq'), may hold values from -6 to 6
- value_vectors: bfloat16 [4, 8192, 1536], P('dp', 'seq'), may hold values from -6 to 6
- features: bfloat16 [4, 8192, 2048], P('dp', 'seq'), may hold values from -6 to 6
- w_level: bfloat16 [2048, 144], replicated, may hold values from -0.125 to 0.125
- offsets: int32 [4, 64], P('dp', 'seq'), may hold values from 0 to 128, as said below
- cotangent: bfloat16 [4, 8192, 1536], P('dp', 'seq'), may hold values from -6 to 6
- final_grad: bfloat16 [4, 12, 128, 128], P('dp'), may hold values from -6 to 6
Outputs:
- normed: bfloat16 [4, 8192, 1536], P('dp', 'seq')
- grad_query: bfloat16 [4, 8192, 1536], P('dp', 'seq')
- grad_key: bfloat16 [4, 8192, 1536], P('dp', 'seq')
- grad_value: bfloat16 [4, 8192, 1536], P('dp', 'seq')
- grad_level: float32 [2048, 144], P('seq')
- final_state: float32 [4, 12, 128, 128], P('dp')
Inputs may be any that keep to these rules, and one draw needn't show every extreme that they name: `offsets`: each stretch of 128 positions holds at most one document start, at the given place; the value 128 means that none starts in the stretch.
All inputs are finite; a program needn't handle non-finite values.
Results may differ from a plain program's by a relative error of at most 0.001.
Values sent between devices are 32-bit elements; how exact they have to be, the bound alone decides.
No kernel may reach another device: no remote copies, remote signals or barrier semaphores. Data moves between devices by JAX's collectives and lax.ppermute only.
A program may use at most 128 MiB of HBM per device.

v0:
```python
import jax
import jax.numpy as jnp
from jax import lax
from jax.experimental import pallas as pl
from jax.experimental.pallas import tpu as pltpu
from jax.sharding import PartitionSpec as P

HEADS = 12
HALF = HEADS // 2
HD = 128
STRETCH = 128
ROWS = 2 * STRETCH
LEVELS = 12
BITS = 5
HROWS = HALF * HD
FROWS = HEADS * HD
SHARE = 64
EPS = 1e-06
SCALE = 0.0625
F32 = jnp.float32
BF16 = jnp.bfloat16

NN = (((1,), (0,)), ((), ()))
NT = (((1,), (1,)), ((), ()))
TN = (((0,), (0,)), ((), ()))


def dot(a, b, dims=NN):
    return lax.dot_general(a, b, dims, preferred_element_type=F32)


def split(a):
    high = a.astype(BF16)
    return high, (a - high.astype(F32)).astype(BF16)


def split3(a):
    high = a.astype(BF16)
    rest = a - high.astype(F32)
    middle = rest.astype(BF16)
    return high, middle, (rest - middle.astype(F32)).astype(BF16)


def lanes(*parts):
    return jnp.concatenate(parts, axis=1)


def rows(*parts):
    return jnp.concatenate(parts, axis=0)


def seq_index():
    return lax.axis_index("seq").astype(jnp.int32)


def bit_of(b):
    return lax.rem(lax.shift_right_logical(seq_index(), b), 2)


def core():
    return bit_of(0)


def chip_x():
    return lax.rem(lax.shift_right_logical(seq_index(), 1), 4)


def chip_z():
    return lax.shift_right_logical(seq_index(), 3)


def sds(shape, dtype=F32):
    return jax.ShapeDtypeStruct(shape, dtype)


def call(kernel, out_shape, *args, scratch=(), flops=0, name=None, smem=()):
    outs = out_shape if isinstance(out_shape, (list, tuple)) else [out_shape]
    size = sum(a.size * a.dtype.itemsize for a in args)
    size += sum(s.size * jnp.dtype(s.dtype).itemsize for s in outs)
    in_specs = [
        pl.BlockSpec(memory_space=pltpu.SMEM if n in smem else pltpu.VMEM) for n in range(len(args))
    ]
    out_specs = [pl.BlockSpec(memory_space=pltpu.VMEM) for _ in outs]
    with jax.named_scope(name):
        return pl.pallas_call(
            kernel,
            in_specs=in_specs,
            out_specs=out_specs if isinstance(out_shape, (list, tuple)) else out_specs[0],
            scratch_shapes=list(scratch),
            out_shape=out_shape,
            compiler_params=pltpu.CompilerParams(vmem_limit_bytes=16 * 2**20),
            cost_estimate=pl.CostEstimate(flops=flops, bytes_accessed=size, transcendentals=0),
            name=name,
        )(*args)


def per_head(step, unroll=2):
    half = core() * HALF

    def own_half(n, carry):
        step(n, half + n, True)
        return carry

    def other_half(n, carry):
        step(n, HALF - half + n, False)
        return carry

    lax.fori_loop(0, HALF, own_half, 0, unroll=unroll)
    lax.fori_loop(0, HALF, other_half, 0, unroll=unroll)


def cut(n):
    return pl.ds(pl.multiple_of(n * HD, HD), HD)


def tails_kernel(off_ref, k_ref, v_ref, o_ref, keys_ref, open_ref, pair_ref):
    off0, off1 = off_ref[0, 0], off_ref[0, 1]
    t = lax.broadcasted_iota(jnp.int32, (ROWS, HD), 0)
    second = t >= STRETCH
    u = jnp.where(second, t - STRETCH, t)
    off = jnp.where(second, off1, off0)
    inside = jnp.where(off < STRETCH, jnp.where(u >= off, 1.0, 0.0), 0.0)
    kept = jnp.where(off < STRETCH, inside, 1.0)
    f0, f1 = (off0 < STRETCH).astype(F32), (off1 < STRETCH).astype(F32)
    keys = kept * jnp.where(second, 1.0, 1.0 - f1)
    keys_ref[...] = keys
    open_ref[...] = (1.0 - inside) * jnp.where(second, 1.0 - f0, 1.0)

    def head(h, carry):
        kept_keys = (k_ref[:, cut(h)].astype(F32) * keys).astype(BF16)
        o_ref[cut(h), :] = dot(kept_keys, v_ref[:, cut(h)], TN)
        return carry

    lax.fori_loop(0, HEADS, head, 0, unroll=3)
    o_ref[FROWS : FROWS + 8, :] = jnp.full((8, HD), jnp.maximum(f0, f1), F32)

    t = lax.broadcasted_iota(jnp.int32, (ROWS, ROWS), 0)
    s = lax.broadcasted_iota(jnp.int32, (ROWS, ROWS), 1)
    t2, s2 = t >= STRETCH, s >= STRETCH
    ut, us = jnp.where(t2, t - STRETCH, t), jnp.where(s2, s - STRETCH, s)
    t_off, s_off = jnp.where(t2, off1, off0), jnp.where(s2, off1, off0)
    t_in = jnp.where(t_off < STRETCH, jnp.where(ut >= t_off, 1, 0), 0)
    s_in = jnp.where(s_off < STRETCH, jnp.where(us >= s_off, 1, 0), 0)
    s_kept = jnp.where(s_off < STRETCH, s_in, 1)
    same = jnp.where(ut >= us, 1, 0) * (1 - t_in * (1 - s_in))
    cross = (1 - t_in) * s_kept * jnp.where(t2, 1, 0)
    both = jnp.where(t2, 1, 0) == jnp.where(s2, 1, 0)
    pair_ref[...] = jnp.where(both, same, cross).astype(F32)


def tails(offsets, k, v):
    return call(
        tails_kernel,
        [sds((FROWS + 8, HD)), sds((ROWS, HD)), sds((ROWS, HD)), sds((ROWS, ROWS))],
        offsets, k, v, flops=2 * ROWS * HD * FROWS, name="tails", smem=(0,),
    )


def joined(own, other, own_flag, other_flag, upper):
    own_by = jnp.where(upper, jnp.ones_like(other_flag), 1.0 - other_flag)
    other_by = jnp.where(upper, 1.0 - own_flag, jnp.ones_like(own_flag))
    return own * own_by + other * other_by


def join_first_kernel(a_ref, b_ref, o_ref):
    upper = core() == 1
    half = pl.ds(pl.multiple_of(core() * HROWS, HROWS), HROWS)
    af, bf = a_ref[FROWS:, :], b_ref[FROWS:, :]
    o_ref[:HROWS, :] = joined(a_ref[half, :], b_ref[half, :], af[0:1], bf[0:1], upper)
    o_ref[HROWS:, :] = jnp.maximum(af, bf)


def join_kernel(bit):
    def kernel(a_ref, b_ref, o_ref):
        upper = bit_of(bit) == 1
        af, bf = a_ref[HROWS:, :], b_ref[HROWS:, :]
        o_ref[:HROWS, :] = joined(a_ref[:HROWS, :], b_ref[:HROWS, :], af[0:1], bf[0:1], upper)
        o_ref[HROWS:, :] = jnp.maximum(af, bf)

    return kernel


def join(own, other, bit):
    kernel = join_kernel(bit) if bit else join_first_kernel
    return call(kernel, sds((HROWS + 8, HD)), own, other, flops=4 * HROWS * HD, name=f"join{bit}")


def gates_kernel(x_ref, w_ref, gate_ref, slope_ref):
    logit = dot(x_ref[...], w_ref[:HD, :], NT)
    gate_ref[...] = jax.nn.softplus(logit)
    slope_ref[...] = 1.0 / (1.0 + jnp.exp(-logit))


def gates(x, w):
    return call(
        gates_kernel, [sds((ROWS, HD))] * 2, x, w, flops=2 * x.size * HD, name="gates"
    )


def head_columns(gate_ref, h):
    return pltpu.roll(gate_ref[...], lax.rem(HD - h, HD), axis=1)


def column(rolled, slot):
    return rolled[:, slot * HEADS : slot * HEADS + 1]


def local_weights(q, k, gate_cols, mask):
    first = lax.broadcasted_iota(jnp.int32, (ROWS, 1), 0) < STRETCH
    g0, g1 = column(gate_cols, 0), column(gate_cols, 1)
    left = jnp.where(first, g0, g1)
    raw = dot(q, k, NT) * mask
    return raw, left, g0, first


def by_columns(a, left, right):
    return lanes(a[:, :HD] * left, a[:, HD:] * right)


def intra_kernel(q_ref, k_ref, v_ref, pair_ref, same_ref, near_ref):
    low, high = slice(0, STRETCH), slice(STRETCH, ROWS)

    def head(h, carry):
        raw = dot(q_ref[:, cut(h)], k_ref[:, cut(h)], NT) * pair_ref[...]
        v0, v1 = v_ref[low, cut(h)], v_ref[high, cut(h)]
        for out, a, v in (
            (same_ref.at[low, cut(h)], raw[low, :HD], v0),
            (same_ref.at[high, cut(h)], raw[high, HD:], v1),
            (near_ref.at[:, cut(h)], raw[high, :HD], v0),
        ):
            out[...] = dot(lanes(*split3(a)), rows(v, v, v))
        return carry

    lax.fori_loop(0, HEADS, head, 0, unroll=2)


def intra(q, k, v, pair):
    return call(
        intra_kernel, [sds((ROWS, FROWS)), sds((STRETCH, FROWS))], q, k, v, pair,
        flops=6 * ROWS * ROWS * FROWS, name="intra",
    )


def usable_rows(flags):
    prefix = jnp.zeros((1, HD), F32)
    result = []
    for b, flag in enumerate(flags):
        upper = bit_of(b).astype(F32)
        result.append(upper * (1.0 - prefix))
        prefix = jnp.maximum(prefix, upper * flag)
    return result


def flag_rows(first_ref, own_refs):
    return [first_ref[FROWS : FROWS + 1, :]] + [r[HROWS : HROWS + 1, :] for r in own_refs]


def level_weight(cols, mask, usable, b):
    return column(cols, 2 + b) * (mask * usable)


def state_products(q, states):
    high, middle, low = zip(*[split3(s) for s in states])
    return dot(lanes(q, q, q), rows(lanes(*high), lanes(*middle), lanes(*low)))


def low_levels_kernel(
    same_ref, near_ref, q_ref, gate_ref, open_ref, s0, a1, a2, a3, o1, o2, o3, mix_ref, p0, p1, p2, p3
):
    usable = usable_rows(flag_rows(s0, (a1, a2, a3)))
    mask = open_ref[...]

    def step(n, h, own):
        cols = head_columns(gate_ref, h)
        refs = (a1, a2, a3) if own else (o1, o2, o3)
        states = [s0[cut(h), :]] + [r[cut(n), :] for r in refs]
        prod = state_products(q_ref[:, cut(h)], states)
        near = column(cols, 1)[STRETCH:] * near_ref[:, cut(h)]
        mixed = column(cols, 0) * same_ref[:, cut(h)] + rows(jnp.zeros((STRETCH, HD), F32), near)
        for b, ref in enumerate((p0, p1, p2, p3)):
            part = prod[:, b * HD : (b + 1) * HD]
            ref[:, cut(h)] = part
            mixed = mixed + level_weight(cols, mask, usable[b], b) * part
        mix_ref[:, cut(h)] = mixed

    per_head(step)


def low_levels(same, near, q, gate, is_open, first, own, other):
    return call(
        low_levels_kernel, [sds((ROWS, FROWS))] * 5, same, near, q, gate, is_open, first, *own,
        *other, flops=16 * ROWS * HD * FROWS, name="low_levels",
    )


def top_level_kernel(
    mix_ref, q_ref, g_ref, gate_ref, open_ref, s0, a1, a2, a3, a4, o4, norm_ref, dsum_ref, p4,
    da4, do4
):
    usable = usable_rows(flag_rows(s0, (a1, a2, a3, a4)))
    mask = open_ref[...]

    def step(n, h, own):
        cols = head_columns(gate_ref, h)
        weight = level_weight(cols, mask, usable[4], 4)
        q = q_ref[:, cut(h)]
        prod = state_products(q, [(a4 if own else o4)[cut(n), :]])
        p4[:, cut(h)] = prod
        mixed = mix_ref[:, cut(h)] + weight * prod
        scale = lax.rsqrt(jnp.mean(mixed * mixed, axis=1, keepdims=True) + EPS)
        normed = mixed * scale
        norm_ref[:, cut(h)] = normed.astype(BF16)
        g = g_ref[:, cut(h)].astype(F32)
        dsum = scale * (g - normed * jnp.mean(g * normed, axis=1, keepdims=True))
        dsum_ref[:, cut(h)] = dsum
        high, low = split(weight * dsum)
        (da4 if own else do4)[cut(n), :] = dot(rows(q, q), rows(high, low), TN)

    per_head(step)


def top_level(mix, q, g, gate, is_open, first, own, other4):
    wide = sds((ROWS, FROWS))
    return call(
        top_level_kernel,
        [sds((ROWS, FROWS), BF16), wide, wide, sds((HROWS, HD)), sds((HROWS, HD))],
        mix, q, g, gate, is_open, first, *own, other4, flops=8 * ROWS * HD * FROWS,
        name="top_level",
    )


def gate_grads_kernel(
    dsum_ref, same_ref, near_ref, p0, p1, p2, p3, p4, slope_ref, open_ref, s0, a1, a2, a3, a4, out
):
    usable = usable_rows(flag_rows(s0, (a1, a2, a3, a4)))
    lane = lax.broadcasted_iota(jnp.int32, (ROWS, HD), 1)
    out[...] = jnp.zeros((ROWS, HD), F32)

    def head(h, carry):
        dsum = dsum_ref[:, cut(h)]
        near = jnp.sum(dsum[STRETCH:] * near_ref[:, cut(h)], axis=1, keepdims=True)
        values = [
            jnp.sum(dsum * same_ref[:, cut(h)], axis=1, keepdims=True),
            rows(jnp.zeros((STRETCH, 1), F32), near),
        ]
        for ref in (p0, p1, p2, p3, p4):
            values.append(jnp.sum(dsum * ref[:, cut(h)], axis=1, keepdims=True))
        spread = out[...]
        for slot, value in enumerate(values):
            spread = jnp.where(lane == slot * HEADS + h, value, spread)
        out[...] = spread
        return carry

    lax.fori_loop(0, HEADS, head, 0, unroll=2)
    factor = slope_ref[...]
    mask = open_ref[...]
    for b in range(BITS):
        start = (2 + b) * HEADS
        at_level = jnp.where(lane >= start, jnp.where(lane < start + HEADS, 1.0, 0.0), 0.0)
        factor = factor * (1.0 - at_level + at_level * (mask * usable[b]))
    out[...] = out[...] * factor


def gate_grads(dsum, same, near, prods, slope, is_open, first, own):
    return call(
        gate_grads_kernel, sds((ROWS, HD)), dsum, same, near, *prods, slope, is_open, first, *own,
        flops=14 * ROWS * FROWS, name="gate_grads",
    )


def state_grads_kernel(
    q_ref, dsum_ref, gate_ref, open_ref, s0, a1, a2, a3, d0, da1, da2, da3, do1, do2, do3
):
    usable = usable_rows(flag_rows(s0, (a1, a2, a3)))
    mask = open_ref[...]

    def step(n, h, own):
        cols = head_columns(gate_ref, h)
        dsum = dsum_ref[:, cut(h)]
        parts = [level_weight(cols, mask, usable[b], b) * dsum for b in range(4)]
        high, low = split(lanes(*parts))
        q = q_ref[:, cut(h)]
        grad = dot(rows(q, q), rows(high, low), TN)
        d0[cut(h), :] = grad[:, :HD]
        for m, ref in enumerate((da1, da2, da3) if own else (do1, do2, do3)):
            ref[cut(n), :] = grad[:, (m + 1) * HD : (m + 2) * HD]

    per_head(step)


def state_grads(q, dsum, gate, is_open, first, own):
    half = sds((HROWS, HD))
    return call(
        state_grads_kernel, [sds((FROWS, HD))] + [half] * 6, q, dsum, gate, is_open, first, *own,
        flops=16 * ROWS * HD * FROWS, name="state_grads",
    )


def back_kernel(bit):
    def kernel(*refs):
        if bit == BITS - 1:
            fg_ref, own_ref, got_ref, b_ref, p_ref, to_ref, keep_ref = refs
            on_first = (lax.shift_right_logical(seq_index(), 1) == 0).astype(F32)
            half = pl.ds(pl.multiple_of(core() * HROWS, HROWS), HROWS)
            w = fg_ref[half, :].astype(F32) * (SCALE * on_first)
        else:
            w1_ref, w2_ref, own_ref, got_ref, b_ref, p_ref, to_ref, keep_ref = refs
            w = w1_ref[...] + w2_ref[...]
        upper = bit_of(bit) == 1
        own_keep = 1.0 - b_ref[HROWS : HROWS + 1, :]
        partner_keep = 1.0 - p_ref[HROWS : HROWS + 1, :]
        one = jnp.ones_like(own_keep)
        grad = (own_ref[...] + got_ref[...]) * upper.astype(F32)
        to_ref[...] = w * jnp.where(upper, own_keep, one) + grad
        keep_ref[...] = w * jnp.where(upper, one, partner_keep)

    return kernel


def back(bit, ws, own, got, block, partner):
    return call(
        back_kernel(bit), [sds((HROWS, HD))] * 2, *ws, own, got, block, partner,
        flops=8 * HROWS * HD, name=f"back{bit}",
    )


def total_kernel(*refs):
    result = refs[0][...]
    for ref in refs[1:-1]:
        result = result + ref[...]
    refs[-1][...] = result


def total(arrays, name):
    return call(total_kernel, sds(arrays[0].shape), *arrays, flops=arrays[0].size, name=name)


def local_kernel(
    q_ref, k_ref, v_ref, dsum_ref, gate_ref, pair_ref, open_ref, s0, a1, a2, a3, a4, o1, o2, o3, o4,
    gq_ref, gk_ref, gv_ref
):
    usable = usable_rows(flag_rows(s0, (a1, a2, a3, a4)))

    def step(n, h, own):
        q, k, v = q_ref[:, cut(h)], k_ref[:, cut(h)], v_ref[:, cut(h)]
        cols = head_columns(gate_ref, h)
        mask = pair_ref[...]
        raw, left, g0, first = local_weights(q, k, cols, mask)
        wh, wl = split(by_columns(raw, left, g0))
        dh, dm, dl = split3(dsum_ref[:, cut(h)])
        dots = dot(lanes(dh, dm, dl), lanes(v, v, v), NT)
        bh, bl = split(by_columns(dots * mask, left, g0))
        grad_q = dot(bh, k) + dot(bl, k)
        gk_ref[:, cut(h)] = dot(bh, q, TN) + dot(bl, q, TN)
        both = dot(wh, lanes(dh, dm), TN)
        gv_ref[:, cut(h)] = both[:, :HD] + both[:, HD:] + dot(wl, dh, TN)

        open_mask = open_ref[...]
        refs = (a1, a2, a3, a4) if own else (o1, o2, o3, o4)
        states = [s0[cut(h), :]] + [r[cut(n), :] for r in refs]
        sh, sl = split(rows(*states))
        back_all = dot(lanes(dh, dh, dm), lanes(sh, sl, sh), NT)
        for b in range(BITS):
            part = back_all[:, b * HD : (b + 1) * HD]
            grad_q = grad_q + level_weight(cols, open_mask, usable[b], b) * part
        gq_ref[:, cut(h)] = grad_q.astype(BF16)

    per_head(step)


def local_grads(q, k, v, dsum, gate, pair, is_open, first, own, other):
    return call(
        local_kernel, [sds((ROWS, FROWS), BF16), sds((ROWS, FROWS)), sds((ROWS, FROWS))],
        q, k, v, dsum, gate, pair, is_open, first, *own, *other, flops=60 * ROWS * HD * FROWS,
        name="local_grads",
    )


def final_kernel(own_ref, other_ref, o_ref):
    start = core() * HROWS
    o_ref[pl.ds(pl.multiple_of(start, HROWS), HROWS), :] = own_ref[:HROWS, :] * SCALE
    o_ref[pl.ds(pl.multiple_of(HROWS - start, HROWS), HROWS), :] = other_ref[:HROWS, :] * SCALE


def final(own, other):
    return call(final_kernel, sds((FROWS, HD)), own, other, flops=FROWS * HD, name="final")


def ends_kernel(k_ref, v_ref, gk_ref, gv_ref, keys_ref, wa, wo, d0, s0, ok_ref, ov_ref):
    lower = core() == 0
    flag = s0[FROWS : FROWS + 1, :]
    keep = jnp.where(lower, 1.0 - flag, jnp.ones_like(flag))
    mask = keys_ref[...]

    def step(n, h, own):
        grad = (wa if own else wo)[cut(n), :] * keep + d0[cut(h), :]
        high, low = split(grad)
        k, v = k_ref[:, cut(h)], v_ref[:, cut(h)]
        by_value = dot(lanes(v, v), lanes(high, low), NT)
        by_key = dot(lanes(k, k), rows(high, low))
        ok_ref[:, cut(h)] = (gk_ref[:, cut(h)] + mask * by_value).astype(BF16)
        ov_ref[:, cut(h)] = (gv_ref[:, cut(h)] + mask * by_key).astype(BF16)

    per_head(step)


def ends(k, v, gk, gv, keys, w_own, w_other, d0, first):
    return call(
        ends_kernel, [sds((ROWS, FROWS), BF16)] * 2, k, v, gk, gv, keys, w_own, w_other, d0, first,
        flops=8 * ROWS * HD * FROWS, name="ends",
    )


def project_kernel(x_ref, d_ref, own_ref, other_ref):
    high, low = split(d_ref[...])
    stacked = rows(high, low)
    first = core() == 0

    def chip(p, carry):
        x = x_ref[:, cut(p)]
        grad = dot(rows(x, x), stacked, TN)
        upper, lower = grad[:SHARE], grad[SHARE:]
        at = pl.ds(pl.multiple_of(p * SHARE, SHARE), SHARE)
        own_ref[at, :] = jnp.where(first, upper, lower)
        other_ref[at, :] = jnp.where(first, lower, upper)
        return carry

    lax.fori_loop(0, 16, chip, 0, unroll=2)


def project(x, dlog):
    return call(
        project_kernel, [sds((16 * SHARE, HD))] * 2, x, dlog, flops=4 * x.size * HD, name="project"
    )


def halve_kernel(side_of, length):
    def kernel(a_ref, b_ref, keep_ref, send_ref):
        side = side_of()
        keep = pl.ds(pl.multiple_of(side * length, length), length)
        send = pl.ds(pl.multiple_of((1 - side) * length, length), length)
        keep_ref[...] = a_ref[keep, :] + b_ref[keep, :]
        send_ref[...] = a_ref[send, :] + b_ref[send, :]

    return kernel


def halve(a, b, bit):
    length = a.shape[0] // 2
    return call(
        halve_kernel(lambda: bit_of(bit), length), [sds((length, HD))] * 2, a, b, flops=a.size,
        name=f"halve{bit}",
    )


def widen_kernel(a_ref, b_ref, o_ref):
    o_ref[:, :HD] = a_ref[...] + b_ref[...]
    o_ref[:, HD:] = jnp.zeros((SHARE, LEVELS * HEADS - HD), F32)


def widen(a, b):
    return call(widen_kernel, sds((SHARE, LEVELS * HEADS)), a, b, flops=1000, name="widen")


FLIP = (0b1, 0b10, 0b110, 0b1000, 0b11000)


def swap(value, bit, name):
    with jax.named_scope(name):
        return lax.ppermute(value, "seq", [(i, i ^ FLIP[bit]) for i in range(32)])


def swap_y(value, flip, name):
    with jax.named_scope(name):
        return lax.ppermute(value, "dp", [(i, i ^ flip) for i in range(4)])


def hold(value, *others):
    return lax.optimization_barrier((value, *others))[0]


def body(queries, key_vectors, value_vectors, features, w_level, offsets, cotangent, final_grad):
    q, k, v, g = (a.reshape(ROWS, FROWS) for a in (queries, key_vectors, value_vectors, cotangent))
    x = features.reshape(ROWS, -1)
    fg = final_grad.reshape(FROWS, HD)

    mine, keys, is_open, pair = tails(offsets, k, v)
    first = swap(mine, 0, "turn0")
    blocks = {1: join(mine, first, 0)}
    own, other = [], []
    for b in range(1, BITS):
        got = swap(blocks[b], b, f"up{b}")
        if b == 1:
            gate, slope = gates(x, w_level.T)
            got = hold(got, gate)
        elif b == 2:
            same, near = intra(q, k, v, pair)
            got = hold(got, same)
        elif b == 4:
            mix, *prods = low_levels(same, near, q, gate, is_open, first, own[:3], other[:3])
            got = hold(got, mix)
        own.append(got)
        other.append(swap(got, 0, f"turn{b}"))
        if b < BITS - 1:
            blocks[b + 1] = join(blocks[b], got, b)

    normed, dsum, prod4, da4, do4 = top_level(mix, q, g, gate, is_open, first, own, other[3])
    d_own, d_other = [None, None, None, da4], [None, None, None, do4]
    ws = [fg]
    for b in reversed(range(1, BITS)):
        got = swap(d_other[b - 1], 0, f"half{b}")
        to_partner, kept = back(b, ws, d_own[b - 1], got, blocks[b], own[b - 1])
        moved = swap(to_partner, b, f"down{b}")
        if b == 4:
            dlog = gate_grads(dsum, same, near, [*prods, prod4], slope, is_open, first, own)
            share, send = project(x, dlog)
            send = swap(send, 0, "share")
            d0, *rest = state_grads(q, hold(dsum, share), gate, is_open, first, own[:3])
            d_own[:3], d_other[:3] = rest[:3], rest[3:]
            moved = hold(moved, d0)
        elif b == 3:
            share, send = halve(share, send, 4)
            send = swap(send, 4, "share4")
            grad_q, gk, gv = local_grads(
                q, k, v, hold(dsum, share), gate, pair, is_open, first, own, other
            )
            moved = hold(moved, gk)
        elif b == 2:
            blocks[5] = join(blocks[4], own[3], 4)
            fin_other = swap(blocks[5], 0, "fin")
            d0_got = lax.ppermute(d0, "seq", [(i + 1, i) for i in range(0, 32, 2)])
            share, send = halve(share, send, 3)
            send = swap(send, 3, "share3")
            share, send = halve(share, send, 2)
            moved = hold(moved, share, blocks[5])
        else:
            send = swap(send, 2, "share2")
            fin = final(blocks[5], fin_other)
            share, send = halve(share, send, 1)
            send = swap(send, 1, "share1")
            moved = hold(moved, share, fin)
        ws = [kept, moved]
    w_own = total(ws, "w_chip")
    w_other = swap(w_own, 0, "half0")

    row = total([share, send], "row")
    row = total([row, swap_y(row, 3, "share_y2")], "row2")
    grad_level = widen(row, swap_y(row, 1, "share_y1"))

    grad_k, grad_v = ends(k, v, gk, gv, keys, w_own, w_other, d0_got, first)
    flat = (1, ROWS, FROWS)
    return (
        normed.reshape(flat),
        grad_q.reshape(flat),
        grad_k.reshape(flat),
        grad_v.reshape(flat),
        grad_level,
        fin.reshape(1, HEADS, HD, HD),
    )


def solution(mesh):
    wide = P("dp", "seq", None)
    state = P("dp", None, None, None)
    return jax.shard_map(
        body,
        mesh=mesh,
        in_specs=(wide, wide, wide, wide, P(), P("dp", "seq"), wide, state),
        out_specs=(wide, wide, wide, wide, P("seq", None), state),
        check_vma=False,
    )
```

profile of v0, /device:TPU:0, one launch (start us, length us, event | category | flops | bytes accessed | tf_op | source)
XLA Modules:
  0.0 135.6 jit_solution(12389522686918060670)
XLA Ops:
  3.6 1.6 %tails.1 = (f32[1544,128]{1,0:T(8,128)S(1)}, f32[256,128]{1,0:T(8,128)S(1)}, f32[256,128]{1,0:T(8,128)S(1)}, f32[256,256]{1,0:T(8,128)S(1)}) custom-call(s32[1,2]{1,0:T(1,128)S(1)} %copy-done.9, bf16[256,1536]{1,0:T(8,128)(2,1)S(1)} %bitcast.17, bf16[256,1536]{1,0:T(8,128)(2,1)S(1)} %bitcast.21), custom_call_target="tpu_custom_call" | custom-call | flops 100663296 | bytes 2887688 | tf_op jit(solution)/shard_map/tails/tails/pallas_call | solution.py:85
  5.3 2.3 %collective-permute-done.b_ref.s0 = f32[1544,128]{1,0:T(8,128)S(1)} collective-permute-done((f32[1544,128]{1,0:T(8,128)S(1)}, f32[1544,128]{1,0:T(8,128)S(1)}, u32[]{:S(2)}, u32[]{:S(2)}) %collective-permute-start) | collective-permute-done | bytes 790560 | tf_op jit(solution)/shard_map/turn0/ppermute | solution.py:570
  7.7 1.7 %collective-permute-start.1 = (f32[776,128]{1,0:T(8,128)S(1)}, f32[776,128]{1,0:T(8,128)S(1)}, u32[]{:S(2)}, u32[]{:S(2)}) collective-permute-start(f32[776,128]{1,0:T(8,128)S(1)} %join0.1.a_ref.refs_4_), channel_id=1, source_target_pairs={{0,8},{4,12},{8,0},{12,4},{16,24},{20,28},{24,16},{28,20},{32,40},... | collective-permute-start | bytes 1191944 | tf_op jit(solution)/shard_map/up1/ppermute | solution.py:570
  9.8 9.2 %collective-permute-done.1.b_ref.a1.refs_5_ = f32[776,128]{1,0:T(8,128)S(1)} collective-permute-done((f32[776,128]{1,0:T(8,128)S(1)}, f32[776,128]{1,0:T(8,128)S(1)}, u32[]{:S(2)}, u32[]{:S(2)}) %collective-permute-start.1) | collective-permute-done | bytes 397344 | tf_op jit(solution)/shard_map/up1/ppermute | solution.py:570
  19.1 2.9 %collective-permute-start.2 = (f32[776,128]{1,0:T(8,128)S(1)}, f32[776,128]{1,0:T(8,128)S(1)}, u32[]{:S(2)}, u32[]{:S(2)}) collective-permute-start(f32[776,128]{1,0:T(8,128)S(1)} %join1.1.a_ref.refs_4_), channel_id=1, source_target_pairs={{0,24},{4,28},{8,16},{12,20},{16,8},{20,12},{24,0},{28,4},{32,56},... | collective-permute-start | bytes 1191944 | tf_op jit(solution)/shard_map/up2/ppermute | solution.py:570
  22.0 3.8 %intra.1 = (f32[256,1536]{1,0:T(8,128)S(1)}, f32[128,1536]{1,0:T(8,128)S(1)}) custom-call(bf16[256,1536]{1,0:T(8,128)(2,1)S(1)} %bitcast.12, bf16[256,1536]{1,0:T(8,128)(2,1)S(1)} %bitcast.18, bf16[256,1536]{1,0:T(8,128)(2,1)S(1)} %bitcast.22, f32[256,256]{1,0:T(8,128)S(1)} %get-tuple-element.63.pair_ref), custom_call_target="tpu_custom_call" | custom-call | flops 603979776 | bytes 4980736 | tf_op jit(solution)/shard_map/intra/intra/pallas_call | solution.py:85
  25.8 4.9 %collective-permute-done.2.b_ref.a2.refs_5_ = f32[776,128]{1,0:T(8,128)S(1)} collective-permute-done((f32[776,128]{1,0:T(8,128)S(1)}, f32[776,128]{1,0:T(8,128)S(1)}, u32[]{:S(2)}, u32[]{:S(2)}) %collective-permute-start.2) | collective-permute-done | bytes 397344 | tf_op jit(solution)/shard_map/up2/ppermute | solution.py:570
  30.8 2.1 %collective-permute-start.3 = (f32[776,128]{1,0:T(8,128)S(1)}, f32[776,128]{1,0:T(8,128)S(1)}, u32[]{:S(2)}, u32[]{:S(2)}) collective-permute-start(f32[776,128]{1,0:T(8,128)S(1)} %join2.1.a_ref.refs_4_), channel_id=1, source_target_pairs={{0,32},{4,36},{8,40},{12,44},{16,48},{20,52},{24,56},{28,60},{32,0... | collective-permute-start | bytes 1191944 | tf_op jit(solution)/shard_map/up3/ppermute | solution.py:570
  33.4 7.3 %collective-permute-done.3.a3.b_ref.refs_5_ = f32[776,128]{1,0:T(8,128)S(1)} collective-permute-done((f32[776,128]{1,0:T(8,128)S(1)}, f32[776,128]{1,0:T(8,128)S(1)}, u32[]{:S(2)}, u32[]{:S(2)}) %collective-permute-start.3) | collective-permute-done | bytes 397344 | tf_op jit(solution)/shard_map/up3/ppermute | solution.py:570
  40.8 3.9 %collective-permute-start.7 = (f32[776,128]{1,0:T(8,128)S(1)}, f32[776,128]{1,0:T(8,128)S(1)}, u32[]{:S(2)}, u32[]{:S(2)}) collective-permute-start(f32[776,128]{1,0:T(8,128)S(1)} %join3.1.refs_3_.a_ref), channel_id=1, source_target_pairs={{0,96},{4,100},{8,104},{12,108},{16,112},{20,116},{24,120},{28,124... | collective-permute-start | bytes 1191944 | tf_op jit(solution)/shard_map/up4/ppermute | solution.py:570
  44.7 5.3 %low_levels.1 = (f32[256,1536]{1,0:T(8,128)S(1)}, f32[256,1536]{1,0:T(8,128)S(1)}, f32[256,1536]{1,0:T(8,128)S(1)}, f32[256,1536]{1,0:T(8,128)S(1)}, f32[256,1536]{1,0:T(8,128)S(1)}) custom-call(f32[256,1536]{1,0:T(8,128)S(1)} %get-tuple-element.64.same_ref, f32[128,1536]{1,0:T(8,128)S(1)} %get-tuple-element.65.near_ref, bf16[256,1536]{1,0:T(8,128)(2,1)S(1)} %bitcast.13, ...), custom_call_target="tpu_custom_call" | custom-call | flops 805306368 | bytes 14446592 | tf_op jit(solution)/shard_map/low_levels/low_levels/pallas_call | solution.py:85
  50.0 4.6 %collective-permute-done.7.a4.refs_4_.b_ref = f32[776,128]{1,0:T(8,128)S(1)} collective-permute-done((f32[776,128]{1,0:T(8,128)S(1)}, f32[776,128]{1,0:T(8,128)S(1)}, u32[]{:S(2)}, u32[]{:S(2)}) %collective-permute-start.7) | collective-permute-done | bytes 397344 | tf_op jit(solution)/shard_map/up4/ppermute | solution.py:570
  54.6 1.7 %collective-permute-done.8.o4 = f32[776,128]{1,0:T(8,128)S(1)} collective-permute-done((f32[776,128]{1,0:T(8,128)S(1)}, f32[776,128]{1,0:T(8,128)S(1)}, u32[]{:S(2)}, u32[]{:S(2)}) %collective-permute-start.8) | collective-permute-done | bytes 397344 | tf_op jit(solution)/shard_map/turn4/ppermute | solution.py:570
  56.3 6.7 %top_level.1 = (bf16[256,1536]{1,0:T(8,128)(2,1)}, f32[256,1536]{1,0:T(8,128)S(1)}, f32[256,1536]{1,0:T(8,128)S(1)}, f32[768,128]{1,0:T(8,128)S(1)}, f32[768,128]{1,0:T(8,128)S(1)}) custom-call(f32[256,1536]{1,0:T(8,128)S(1)} %get-tuple-element.71.mix_ref, bf16[256,1536]{1,0:T(8,128)(2,1)S(1)} %bitcast.14, bf16[256,1536]{1,0:T(8,128)(2,1)S(1)} %bitcast.27, ...), custom_call_target="tpu_custom_call" | custom-call | flops 402653184 | bytes 10903552 | tf_op jit(solution)/shard_map/top_level/top_level/pallas_call | solution.py:85
  63.2 3.7 %gate_grads.1.d_ref = f32[256,128]{1,0:T(8,128)S(1)} custom-call(f32[256,1536]{1,0:T(8,128)S(1)} %get-tuple-element.93.dsum_ref, f32[256,1536]{1,0:T(8,128)S(1)} %get-tuple-element.64.same_ref, f32[128,1536]{1,0:T(8,128)S(1)} %get-tuple-element.65.near_ref, f32[256,1536]{1,0:T(8,128)S(1)} %get-tuple-element.75.p0, f32[256,1536]{1,0:T(8,128)S(1)} %get-tuple-element.76.p1, ...), custom_call_target="tpu_custom_call" | custom-call | flops 5505024 | bytes 14569472 | tf_op jit(solution)/shard_map/gate_grads/gate_grads/pallas_call | solution.py:85
  66.8 2.1 %project.1 = (f32[1024,128]{1,0:T(8,128)S(1)}, f32[1024,128]{1,0:T(8,128)S(1)}) custom-call(bf16[256,2048]{1,0:T(8,128)(2,1)S(1)} %bitcast.26, f32[256,128]{1,0:T(8,128)S(1)} %gate_grads.1.d_ref), custom_call_target="tpu_custom_call" | custom-call | flops 268435456 | bytes 2228224 | tf_op jit(solution)/shard_map/project/project/pallas_call | solution.py:85
  69.5 3.0 %collective-permute-start.11 = (f32[768,128]{1,0:T(8,128)S(1)}, f32[768,128]{1,0:T(8,128)S(1)}, u32[]{:S(2)}, u32[]{:S(2)}) collective-permute-start(f32[768,128]{1,0:T(8,128)S(1)} %get-tuple-element.92), channel_id=1, source_target_pairs={{0,96},{4,100},{8,104},{12,108},{16,112},{20,116},{24,120},{28,124... | collective-permute-start | bytes 1179656 | tf_op jit(solution)/shard_map/down4/ppermute | solution.py:570
  72.5 4.8 %state_grads.1 = (f32[1536,128]{1,0:T(8,128)S(1)}, f32[768,128]{1,0:T(8,128)S(1)}, f32[768,128]{1,0:T(8,128)S(1)}, f32[768,128]{1,0:T(8,128)S(1)}, f32[768,128]{...) custom-call(bf16[256,1536]{1,0:T(8,128)(2,1)S(1)} %bitcast.15, ...), custom_call_target="tpu_custom_call" | custom-call | flops 805306368 | bytes 7749632 | tf_op jit(solution)/shard_map/state_grads/state_grads/pallas_call | solution.py:85
  77.4 4.5 %collective-permute-done.11.refs_1_ = f32[768,128]{1,0:T(8,128)S(1)} collective-permute-done((f32[768,128]{1,0:T(8,128)S(1)}, f32[768,128]{1,0:T(8,128)S(1)}, u32[]{:S(2)}, u32[]{:S(2)}) %collective-permute-start.11) | collective-permute-done | bytes 393248 | tf_op jit(solution)/shard_map/down4/ppermute | solution.py:570
  82.4 3.2 %collective-permute-start.16 = (f32[512,128]{1,0:T(8,128)S(1)}, f32[512,128]{1,0:T(8,128)S(1)}, u32[]{:S(2)}, u32[]{:S(2)}) collective-permute-start(f32[512,128]{1,0:T(8,128)S(1)} %get-tuple-element.105), channel_id=1, source_target_pairs={{0,96},{4,100},{8,104},{12,108},{16,112},{20,116},{24,120},{28,124... | collective-permute-start | bytes 786440 | tf_op jit(solution)/shard_map/share4/ppermute | solution.py:570
  85.6 10.0 %local_grads.1 = (bf16[256,1536]{1,0:T(8,128)(2,1)}, f32[256,1536]{1,0:T(8,128)S(1)}, f32[256,1536]{1,0:T(8,128)S(1)}) custom-call(bf16[256,1536]{1,0:T(8,128)(2,1)S(1)} %bitcast.16, bf16[256,1536]{1,0:T(8,128)(2,1)S(1)} %bitcast.19, bf16[256,1536]{1,0:T(8,128)(2,1)S(1)} %bitcast.23, f32[256,1536]{1,0:T(8,128)S(1)} %get-tuple-element.93.dsum_ref, ...), custom_call_target="tpu_custom_call" | custom-call | flops 3019898880 | bytes 12357632 | tf_op jit(solution)/shard_map/local_grads/local_grads/pallas_call | solution.py:85
  95.8 2.8 %collective-permute-start.15 = (f32[768,128]{1,0:T(8,128)S(1)}, f32[768,128]{1,0:T(8,128)S(1)}, u32[]{:S(2)}, u32[]{:S(2)}) collective-permute-start(f32[768,128]{1,0:T(8,128)S(1)} %get-tuple-element.104), channel_id=1, source_target_pairs={{0,24},{4,28},{8,16},{12,20},{16,8},{20,12},{24,0},{28,4},{32,56},... | collective-permute-start | bytes 1179656 | tf_op jit(solution)/shard_map/down2/ppermute | solution.py:570
  100.4 4.2 %collective-permute-done.17.b_ref = f32[256,128]{1,0:T(8,128)S(1)} collective-permute-done((f32[256,128]{1,0:T(8,128)S(1)}, f32[256,128]{1,0:T(8,128)S(1)}, u32[]{:S(2)}, u32[]{:S(2)}) %collective-permute-start.17) | collective-permute-done | bytes 131104 | tf_op jit(solution)/shard_map/share3/ppermute | solution.py:570
  104.6 3.6 %collective-permute-done.15.refs_1_ = f32[768,128]{1,0:T(8,128)S(1)} collective-permute-done((f32[768,128]{1,0:T(8,128)S(1)}, f32[768,128]{1,0:T(8,128)S(1)}, u32[]{:S(2)}, u32[]{:S(2)}) %collective-permute-start.15) | collective-permute-done | bytes 393248 | tf_op jit(solution)/shard_map/down2/ppermute | solution.py:570
  109.8 2.8 %collective-permute-start.20 = (f32[128,128]{1,0:T(8,128)S(1)}, f32[128,128]{1,0:T(8,128)S(1)}, u32[]{:S(2)}, u32[]{:S(2)}) collective-permute-start(f32[128,128]{1,0:T(8,128)S(1)} %get-tuple-element.114), channel_id=1, source_target_pairs={{0,24},{4,28},{8,16},{12,20},{16,8},{20,12},{24,0},{28,4},{32,56},... | collective-permute-start | bytes 196616 | tf_op jit(solution)/shard_map/share2/ppermute | solution.py:570
  113.5 2.3 %collective-permute-done.20.b_ref = f32[128,128]{1,0:T(8,128)S(1)} collective-permute-done((f32[128,128]{1,0:T(8,128)S(1)}, f32[128,128]{1,0:T(8,128)S(1)}, u32[]{:S(2)}, u32[]{:S(2)}) %collective-permute-start.20) | collective-permute-done | bytes 65568 | tf_op jit(solution)/shard_map/share2/ppermute | solution.py:570
  115.8 3.0 %collective-permute-done.19.refs_1_ = f32[768,128]{1,0:T(8,128)S(1)} collective-permute-done((f32[768,128]{1,0:T(8,128)S(1)}, f32[768,128]{1,0:T(8,128)S(1)}, u32[]{:S(2)}, u32[]{:S(2)}) %collective-permute-start.19) | collective-permute-done | bytes 393248 | tf_op jit(solution)/shard_map/down1/ppermute | solution.py:570
  119.3 3.6 %collective-permute-done.24.refs_1_ = f32[64,128]{1,0:T(8,128)S(1)} collective-permute-done((f32[64,128]{1,0:T(8,128)S(1)}, f32[64,128]{1,0:T(8,128)S(1)}, u32[]{:S(2)}, u32[]{:S(2)}) %collective-permute-start.24) | collective-permute-done | bytes 32800 | tf_op jit(solution)/shard_map/share1/ppermute | solution.py:570
  122.9 3.0 %collective-permute-start.25 = (f32[64,128]{1,0:T(8,128)S(1)}, f32[64,128]{1,0:T(8,128)S(1)}, u32[]{:S(2)}, u32[]{:S(2)}) collective-permute-start(f32[64,128]{1,0:T(8,128)S(1)} %row.1.refs_0_), channel_id=1, source_target_pairs={{0,3},{1,2},{2,1},{3,0},{4,7},{5,6},{6,5},{7,4},{8,11},{9,10},{10,... | collective-permute-start | bytes 98312 | tf_op jit(solution)/shard_map/share_y2/ppermute | solution.py:575
  125.9 2.1 %collective-permute-done.25.refs_1_ = f32[64,128]{1,0:T(8,128)S(1)} collective-permute-done((f32[64,128]{1,0:T(8,128)S(1)}, f32[64,128]{1,0:T(8,128)S(1)}, u32[]{:S(2)}, u32[]{:S(2)}) %collective-permute-start.25) | collective-permute-done | bytes 32800 | tf_op jit(solution)/shard_map/share_y2/ppermute | solution.py:575
  128.4 3.6 %collective-permute-done.26.b_ref = f32[64,128]{1,0:T(8,128)S(1)} collective-permute-done((f32[64,128]{1,0:T(8,128)S(1)}, f32[64,128]{1,0:T(8,128)S(1)}, u32[]{:S(2)}, u32[]{:S(2)}) %collective-permute-start.26) | collective-permute-done | bytes 32800 | tf_op jit(solution)/shard_map/share_y1/ppermute | solution.py:575
  132.6 2.9 %ends.1 = (bf16[256,1536]{1,0:T(8,128)(2,1)}, bf16[256,1536]{1,0:T(8,128)(2,1)}) custom-call(bf16[256,1536]{1,0:T(8,128)(2,1)S(1)} %bitcast.20, bf16[256,1536]{1,0:T(8,128)(2,1)S(1)} %bitcast.24, f32[256,1536]{1,0:T(8,128)S(1)} %get-tuple-element.86.gk_ref, f32[256,1536]{1,0:T(8,128)S(1)} %get-tuple-element.87.gv_ref, ...), custom_call_target="tpu_custom_call" | custom-call | flops 402653184 | bytes 8785920 | tf_op jit(solution)/shard_map/ends/ends/pallas_call | solution.py:85
  (70 shorter events, 11.4 us)
Async XLA Ops:
  5.2 2.4 %collective-permute-start = (f32[1544,128]{1,0:T(8,128)S(1)}, f32[1544,128]{1,0:T(8,128)S(1)}, u32[]{:S(2)}, u32[]{:S(2)}) collective-permute-start(f32[1544,128]{1,0:T(8,128)S(1)} %get-tuple-element.68.a_ref), channel_id=1, source_target_pairs={{0,4},{4,0},{8,12},{12,8},{16,20},{20,16},{24,28},{28,24},{32,36},... | collective-permute-start | bytes 2371592 | tf_op jit(solution)/shard_map/turn0/ppermute | solution.py:570
  7.6 14.4 %copy-start = (bf16[1,256,1536]{2,1,0:T(8,128)(2,1)S(1)}, bf16[1,256,1536]{2,1,0:T(8,128)(2,1)}, u32[]{:S(2)}) copy-start(bf16[1,256,1536]{2,1,0:T(8,128)(2,1)} %param.8) | copy-start | bytes 2359300
  7.7 14.4 %copy-start.2 = (bf16[1,256,1536]{2,1,0:T(8,128)(2,1)S(1)}, bf16[1,256,1536]{2,1,0:T(8,128)(2,1)}, u32[]{:S(2)}) copy-start(bf16[1,256,1536]{2,1,0:T(8,128)(2,1)} %param.9) | copy-start | bytes 2359300
  7.7 14.3 %copy-start.4 = (bf16[1,256,1536]{2,1,0:T(8,128)(2,1)S(1)}, bf16[1,256,1536]{2,1,0:T(8,128)(2,1)}, u32[]{:S(2)}) copy-start(bf16[1,256,1536]{2,1,0:T(8,128)(2,1)} %param.10) | copy-start | bytes 2359300
  7.7 11.3 %collective-permute-start.1 = (f32[776,128]{1,0:T(8,128)S(1)}, f32[776,128]{1,0:T(8,128)S(1)}, u32[]{:S(2)}, u32[]{:S(2)}) collective-permute-start(f32[776,128]{1,0:T(8,128)S(1)} %join0.1.a_ref.refs_4_), channel_id=1, source_target_pairs={{0,8},{4,12},{8,0},{12,4},{16,24},{20,28},{24,16},{28,20},{32,40},... | collective-permute-start | bytes 1191944 | tf_op jit(solution)/shard_map/up1/ppermute | solution.py:570
  19.1 11.7 %collective-permute-start.2 = (f32[776,128]{1,0:T(8,128)S(1)}, f32[776,128]{1,0:T(8,128)S(1)}, u32[]{:S(2)}, u32[]{:S(2)}) collective-permute-start(f32[776,128]{1,0:T(8,128)S(1)} %join1.1.a_ref.refs_4_), channel_id=1, source_target_pairs={{0,24},{4,28},{8,16},{12,20},{16,8},{20,12},{24,0},{28,4},{32,56},... | collective-permute-start | bytes 1191944 | tf_op jit(solution)/shard_map/up2/ppermute | solution.py:570
  30.8 9.9 %collective-permute-start.3 = (f32[776,128]{1,0:T(8,128)S(1)}, f32[776,128]{1,0:T(8,128)S(1)}, u32[]{:S(2)}, u32[]{:S(2)}) collective-permute-start(f32[776,128]{1,0:T(8,128)S(1)} %join2.1.a_ref.refs_4_), channel_id=1, source_target_pairs={{0,32},{4,36},{8,40},{12,44},{16,48},{20,52},{24,56},{28,60},{32,0... | collective-permute-start | bytes 1191944 | tf_op jit(solution)/shard_map/up3/ppermute | solution.py:570
  32.9 11.8 %collective-permute-start.4 = (f32[776,128]{1,0:T(8,128)S(1)}, f32[776,128]{1,0:T(8,128)S(1)}, u32[]{:S(2)}, u32[]{:S(2)}) collective-permute-start(f32[776,128]{1,0:T(8,128)S(1)} %collective-permute-done.1.b_ref.a1.refs_5_), channel_id=1, source_target_pairs={{0,4},{4,0},{8,12},{12,8},{16,20},{20,16},{24,28},{28,24},{32,36},... | collective-permute-start | bytes 1191944 | tf_op jit(solution)/shard_map/turn1/ppermute | solution.py:570
  32.9 11.8 %collective-permute-start.5 = (f32[776,128]{1,0:T(8,128)S(1)}, f32[776,128]{1,0:T(8,128)S(1)}, u32[]{:S(2)}, u32[]{:S(2)}) collective-permute-start(f32[776,128]{1,0:T(8,128)S(1)} %collective-permute-done.2.b_ref.a2.refs_5_), channel_id=1, source_target_pairs={{0,4},{4,0},{8,12},{12,8},{16,20},{20,16},{24,28},{28,24},{32,36},... | collective-permute-start | bytes 1191944 | tf_op jit(solution)/shard_map/turn2/ppermute | solution.py:570
  40.7 4.0 %collective-permute-start.6 = (f32[776,128]{1,0:T(8,128)S(1)}, f32[776,128]{1,0:T(8,128)S(1)}, u32[]{:S(2)}, u32[]{:S(2)}) collective-permute-start(f32[776,128]{1,0:T(8,128)S(1)} %collective-permute-done.3.a3.b_ref.refs_5_), channel_id=1, source_target_pairs={{0,4},{4,0},{8,12},{12,8},{16,20},{20,16},{24,28},{28,24},{32,36},... | collective-permute-start | bytes 1191944 | tf_op jit(solution)/shard_map/turn3/ppermute | solution.py:570
  40.8 13.8 %collective-permute-start.7 = (f32[776,128]{1,0:T(8,128)S(1)}, f32[776,128]{1,0:T(8,128)S(1)}, u32[]{:S(2)}, u32[]{:S(2)}) collective-permute-start(f32[776,128]{1,0:T(8,128)S(1)} %join3.1.refs_3_.a_ref), channel_id=1, source_target_pairs={{0,96},{4,100},{8,104},{12,108},{16,112},{20,116},{24,120},{28,124... | collective-permute-start | bytes 1191944 | tf_op jit(solution)/shard_map/up4/ppermute | solution.py:570
  44.7 11.6 %copy-start.6 = (bf16[1,256,1536]{2,1,0:T(8,128)(2,1)S(1)}, bf16[1,256,1536]{2,1,0:T(8,128)(2,1)}, u32[]{:S(2)}) copy-start(bf16[1,256,1536]{2,1,0:T(8,128)(2,1)} %param.14) | copy-start | bytes 2359300
  54.6 1.7 %collective-permute-start.8 = (f32[776,128]{1,0:T(8,128)S(1)}, f32[776,128]{1,0:T(8,128)S(1)}, u32[]{:S(2)}, u32[]{:S(2)}) collective-permute-start(f32[776,128]{1,0:T(8,128)S(1)} %collective-permute-done.7.a4.refs_4_.b_ref), channel_id=1, source_target_pairs={{0,4},{4,0},{8,12},{12,8},{16,20},{20,16},{24,28},{28,24},{32,36},... | collective-permute-start | bytes 1191944 | tf_op jit(solution)/shard_map/turn4/ppermute | solution.py:570
  63.0 6.3 %collective-permute-start.10 = (f32[768,128]{1,0:T(8,128)S(1)}, f32[768,128]{1,0:T(8,128)S(1)}, u32[]{:S(2)}, u32[]{:S(2)}) collective-permute-start(f32[768,128]{1,0:T(8,128)S(1)} %get-tuple-element.90), channel_id=1, source_target_pairs={{0,4},{4,0},{8,12},{12,8},{16,20},{20,16},{24,28},{28,24},{32,36},... | collective-permute-start | bytes 1179656 | tf_op jit(solution)/shard_map/half4/ppermute | solution.py:570
  63.2 6.2 %copy-start.8 = (bf16[1,12,128,128]{3,2,1,0:T(8,128)(2,1)S(1)}, bf16[1,12,128,128]{3,2,1,0:T(8,128)(2,1)}, u32[]{:S(2)}) copy-start(bf16[1,12,128,128]{3,2,1,0:T(8,128)(2,1)} %param.15) | copy-start | bytes 1179652
  68.9 13.4 %collective-permute-start.9 = (f32[1024,128]{1,0:T(8,128)S(1)}, f32[1024,128]{1,0:T(8,128)S(1)}, u32[]{:S(2)}, u32[]{:S(2)}) collective-permute-start(f32[1024,128]{1,0:T(8,128)S(1)} %get-tuple-element.82), channel_id=1, source_target_pairs={{0,4},{4,0},{8,12},{12,8},{16,20},{20,16},{24,28},{28,24},{32,36},... | collective-permute-start | bytes 1572872 | tf_op jit(solution)/shard_map/share/ppermute | solution.py:570
  69.5 12.5 %collective-permute-start.11 = (f32[768,128]{1,0:T(8,128)S(1)}, f32[768,128]{1,0:T(8,128)S(1)}, u32[]{:S(2)}, u32[]{:S(2)}) collective-permute-start(f32[768,128]{1,0:T(8,128)S(1)} %get-tuple-element.92), channel_id=1, source_target_pairs={{0,96},{4,100},{8,104},{12,108},{16,112},{20,116},{24,120},{28,124... | collective-permute-start | bytes 1179656 | tf_op jit(solution)/shard_map/down4/ppermute | solution.py:570
  77.3 4.6 %collective-permute-start.12 = (f32[768,128]{1,0:T(8,128)S(1)}, f32[768,128]{1,0:T(8,128)S(1)}, u32[]{:S(2)}, u32[]{:S(2)}) collective-permute-start(f32[768,128]{1,0:T(8,128)S(1)} %get-tuple-element.97), channel_id=1, source_target_pairs={{0,4},{4,0},{8,12},{12,8},{16,20},{20,16},{24,28},{28,24},{32,36},... | collective-permute-start | bytes 1179656 | tf_op jit(solution)/shard_map/half3/ppermute | solution.py:570
  82.1 13.5 %collective-permute-start.13 = (f32[768,128]{1,0:T(8,128)S(1)}, f32[768,128]{1,0:T(8,128)S(1)}, u32[]{:S(2)}, u32[]{:S(2)}) collective-permute-start(f32[768,128]{1,0:T(8,128)S(1)} %get-tuple-element.99), channel_id=1, source_target_pairs={{0,32},{4,36},{8,40},{12,44},{16,48},{20,52},{24,56},{28,60},{32,0... | collective-permute-start | bytes 1179656 | tf_op jit(solution)/shard_map/down3/ppermute | solution.py:570
  82.2 13.5 %collective-permute-start.14 = (f32[768,128]{1,0:T(8,128)S(1)}, f32[768,128]{1,0:T(8,128)S(1)}, u32[]{:S(2)}, u32[]{:S(2)}) collective-permute-start(f32[768,128]{1,0:T(8,128)S(1)} %get-tuple-element.102), channel_id=1, source_target_pairs={{0,4},{4,0},{8,12},{12,8},{16,20},{20,16},{24,28},{28,24},{32,36},... | collective-permute-start | bytes 1179656 | tf_op jit(solution)/shard_map/half2/ppermute | solution.py:570
  82.4 16.2 %collective-permute-start.16 = (f32[512,128]{1,0:T(8,128)S(1)}, f32[512,128]{1,0:T(8,128)S(1)}, u32[]{:S(2)}, u32[]{:S(2)}) collective-permute-start(f32[512,128]{1,0:T(8,128)S(1)} %get-tuple-element.105), channel_id=1, source_target_pairs={{0,96},{4,100},{8,104},{12,108},{16,112},{20,116},{24,120},{28,124... | collective-permute-start | bytes 786440 | tf_op jit(solution)/shard_map/share4/ppermute | solution.py:570
  95.8 12.5 %collective-permute-start.15 = (f32[768,128]{1,0:T(8,128)S(1)}, f32[768,128]{1,0:T(8,128)S(1)}, u32[]{:S(2)}, u32[]{:S(2)}) collective-permute-start(f32[768,128]{1,0:T(8,128)S(1)} %get-tuple-element.104), channel_id=1, source_target_pairs={{0,24},{4,28},{8,16},{12,20},{16,8},{20,12},{24,0},{28,4},{32,56},... | collective-permute-start | bytes 1179656 | tf_op jit(solution)/shard_map/down2/ppermute | solution.py:570
  98.6 9.7 %collective-permute-start.18 = (f32[768,128]{1,0:T(8,128)S(1)}, f32[768,128]{1,0:T(8,128)S(1)}, u32[]{:S(2)}, u32[]{:S(2)}) collective-permute-start(f32[768,128]{1,0:T(8,128)S(1)} %get-tuple-element.111), channel_id=1, source_target_pairs={{0,4},{4,0},{8,12},{12,8},{16,20},{20,16},{24,28},{28,24},{32,36},... | collective-permute-start | bytes 1179656 | tf_op jit(solution)/shard_map/half1/ppermute | solution.py:570
  98.6 6.0 %collective-permute-start.17 = (f32[256,128]{1,0:T(8,128)S(1)}, f32[256,128]{1,0:T(8,128)S(1)}, u32[]{:S(2)}, u32[]{:S(2)}) collective-permute-start(f32[256,128]{1,0:T(8,128)S(1)} %get-tuple-element.107), channel_id=1, source_target_pairs={{0,32},{4,36},{8,40},{12,44},{16,48},{20,52},{24,56},{28,60},{32,0... | collective-permute-start | bytes 393224 | tf_op jit(solution)/shard_map/share3/ppermute | solution.py:570
  100.1 12.5 %collective-permute-start.21 = (f32[776,128]{1,0:T(8,128)S(1)}, f32[776,128]{1,0:T(8,128)S(1)}, u32[]{:S(2)}, u32[]{:S(2)}) collective-permute-start(f32[776,128]{1,0:T(8,128)S(1)} %join4.1.own_ref), channel_id=1, source_target_pairs={{0,4},{4,0},{8,12},{12,8},{16,20},{20,16},{24,28},{28,24},{32,36},... | collective-permute-start | bytes 1191944 | tf_op jit(solution)/shard_map/fin/ppermute | solution.py:570
  108.4 10.4 %collective-permute-start.19 = (f32[768,128]{1,0:T(8,128)S(1)}, f32[768,128]{1,0:T(8,128)S(1)}, u32[]{:S(2)}, u32[]{:S(2)}) collective-permute-start(f32[768,128]{1,0:T(8,128)S(1)} %get-tuple-element.113), channel_id=1, source_target_pairs={{0,8},{4,12},{8,0},{12,4},{16,24},{20,28},{24,16},{28,20},{32,40},... | collective-permute-start | bytes 1179656 | tf_op jit(solution)/shard_map/down1/ppermute | solution.py:570
  108.5 24.2 %collective-permute-start.23 = (f32[1536,128]{1,0:T(8,128)S(1)}, f32[1536,128]{1,0:T(8,128)S(1)}, u32[]{:S(2)}, u32[]{:S(2)}) collective-permute-start(f32[1536,128]{1,0:T(8,128)S(1)} %get-tuple-element.94), channel_id=1, source_target_pairs={{4,0},{12,8},{20,16},{28,24},{36,32},{44,40},{52,48},{60,56},{68,6... | collective-permute-start | bytes 2359304 | tf_op jit(solution)/shard_map/ppermute | solution.py:631
  109.8 6.1 %collective-permute-start.20 = (f32[128,128]{1,0:T(8,128)S(1)}, f32[128,128]{1,0:T(8,128)S(1)}, u32[]{:S(2)}, u32[]{:S(2)}) collective-permute-start(f32[128,128]{1,0:T(8,128)S(1)} %get-tuple-element.114), channel_id=1, source_target_pairs={{0,24},{4,28},{8,16},{12,20},{16,8},{20,12},{24,0},{28,4},{32,56},... | collective-permute-start | bytes 196616 | tf_op jit(solution)/shard_map/share2/ppermute | solution.py:570
  118.8 13.8 %collective-permute-start.22 = (f32[768,128]{1,0:T(8,128)S(1)}, f32[768,128]{1,0:T(8,128)S(1)}, u32[]{:S(2)}, u32[]{:S(2)}) collective-permute-start(f32[768,128]{1,0:T(8,128)S(1)} %w_chip.1.wa), channel_id=1, source_target_pairs={{0,4},{4,0},{8,12},{12,8},{16,20},{20,16},{24,28},{28,24},{32,36},... | collective-permute-start | bytes 1179656 | tf_op jit(solution)/shard_map/half0/ppermute | solution.py:570
  118.9 4.0 %collective-permute-start.24 = (f32[64,128]{1,0:T(8,128)S(1)}, f32[64,128]{1,0:T(8,128)S(1)}, u32[]{:S(2)}, u32[]{:S(2)}) collective-permute-start(f32[64,128]{1,0:T(8,128)S(1)} %get-tuple-element.119), channel_id=1, source_target_pairs={{0,8},{4,12},{8,0},{12,4},{16,24},{20,28},{24,16},{28,20},{32,40},... | collective-permute-start | bytes 98312 | tf_op jit(solution)/shard_map/share1/ppermute | solution.py:570
  122.9 5.1 %collective-permute-start.25 = (f32[64,128]{1,0:T(8,128)S(1)}, f32[64,128]{1,0:T(8,128)S(1)}, u32[]{:S(2)}, u32[]{:S(2)}) collective-permute-start(f32[64,128]{1,0:T(8,128)S(1)} %row.1.refs_0_), channel_id=1, source_target_pairs={{0,3},{1,2},{2,1},{3,0},{4,7},{5,6},{6,5},{7,4},{8,11},{9,10},{10,... | collective-permute-start | bytes 98312 | tf_op jit(solution)/shard_map/share_y2/ppermute | solution.py:575
  128.1 3.9 %collective-permute-start.26 = (f32[64,128]{1,0:T(8,128)S(1)}, f32[64,128]{1,0:T(8,128)S(1)}, u32[]{:S(2)}, u32[]{:S(2)}) collective-permute-start(f32[64,128]{1,0:T(8,128)S(1)} %row2.1.a_ref), channel_id=1, source_target_pairs={{0,1},{1,0},{2,3},{3,2},{4,5},{5,4},{6,7},{7,6},{8,9},{9,8},{10,11... | collective-permute-start | bytes 98312 | tf_op jit(solution)/shard_map/share_y1/ppermute | solution.py:575
  (5 other events, 14.5 us)
where the time goes:
time: 136 us
  waiting for transfers between devices  56.9 us (42%)
  Pallas kernels  44 us (32%)
  starting transfers between devices  30.9 us (23%)
  local copies, waits for them, and re-layouts  2.95 us (2%)
    ppermute x24, waiting for transfers between devices, swap(): return lax.ppermute(value, 'seq', [(i, i ^ FLIP[bit]) for i in range(32)])  51.2 us
    pallas_call x28, Pallas kernels, call(): pl.pallas_call(kernel, in_specs=in_specs, out_specs=out_specs if isinstan...  44 us
    ppermute x24, starting transfers between devices, swap(): return lax.ppermute(value, 'seq', [(i, i ^ FLIP[bit]) for i in range(32)])  26.2 us
    ppermute x2, waiting for transfers between devices, swap_y(): return lax.ppermute(value, 'dp', [(i, i ^ flip) for i in range(4)])  5.69 us
    ppermute x2, starting transfers between devices, swap_y(): return lax.ppermute(value, 'dp', [(i, i ^ flip) for i in range(4)])  3.35 us
    unnamed x20, local copies, waits for them, and re-layouts  2.95 us
  transfers between devices with their start and end apart: 27, of which 14 were waited for; matrix products, arithmetic and copies ran while one was open for 0% of the time, Pallas kernels for 24%

commit v1 on v0

--- a/solution.py
+++ b/solution.py
@@ -1,3 +1,5 @@
+import functools
+
 import jax
 import jax.numpy as jnp
 from jax import lax
@@ -94,7 +96,7 @@
         )(*args)
 
 
-def per_head(step, unroll=2):
+def per_head(step, unroll=2, own=True, other=True):
     half = core() * HALF
 
     def own_half(n, carry):
@@ -105,8 +107,10 @@
         step(n, HALF - half + n, False)
         return carry
 
-    lax.fori_loop(0, HALF, own_half, 0, unroll=unroll)
-    lax.fori_loop(0, HALF, other_half, 0, unroll=unroll)
+    if own:
+        lax.fori_loop(0, HALF, own_half, 0, unroll=unroll)
+    if other:
+        lax.fori_loop(0, HALF, other_half, 0, unroll=unroll)
 
 
 def cut(n):
@@ -293,10 +297,9 @@
     )
 
 
-def top_level_kernel(
-    mix_ref, q_ref, g_ref, gate_ref, open_ref, s0, a1, a2, a3, a4, o4, norm_ref, dsum_ref, p4,
-    da4, do4
-):
+def top_level_kernel(own_half, *refs):
+    mix_ref, q_ref, g_ref, gate_ref, open_ref, s0, a1, a2, a3, a4, state = refs[:11]
+    norm_ref, dsum_ref, p4, grad_ref = refs[-4:]
     usable = usable_rows(flag_rows(s0, (a1, a2, a3, a4)))
     mask = open_ref[...]
 
@@ -304,54 +307,61 @@
         cols = head_columns(gate_ref, h)
         weight = level_weight(cols, mask, usable[4], 4)
         q = q_ref[:, cut(h)]
-        prod = state_products(q, [(a4 if own else o4)[cut(n), :]])
-        p4[:, cut(h)] = prod
+        prod = state_products(q, [state[cut(n), :]])
+        p4[:, cut(n)] = prod
         mixed = mix_ref[:, cut(h)] + weight * prod
         scale = lax.rsqrt(jnp.mean(mixed * mixed, axis=1, keepdims=True) + EPS)
         normed = mixed * scale
-        norm_ref[:, cut(h)] = normed.astype(BF16)
+        norm_ref[:, cut(n if own_half else h)] = normed.astype(BF16)
         g = g_ref[:, cut(h)].astype(F32)
         dsum = scale * (g - normed * jnp.mean(g * normed, axis=1, keepdims=True))
-        dsum_ref[:, cut(h)] = dsum
+        dsum_ref[:, cut(n)] = dsum
         high, low = split(weight * dsum)
-        (da4 if own else do4)[cut(n), :] = dot(rows(q, q), rows(high, low), TN)
-
-    per_head(step)
-
-
-def top_level(mix, q, g, gate, is_open, first, own, other4):
-    wide = sds((ROWS, FROWS))
-    return call(
-        top_level_kernel,
-        [sds((ROWS, FROWS), BF16), wide, wide, sds((HROWS, HD)), sds((HROWS, HD))],
-        mix, q, g, gate, is_open, first, *own, other4, flops=8 * ROWS * HD * FROWS,
-        name="top_level",
+        grad_ref[cut(n), :] = dot(rows(q, q), rows(high, low), TN)
+        if not own_half:
+            norm_ref[:, cut(HALF * core() + n)] = refs[11][:, cut(n)]
+
+    per_head(step, own=own_half, other=not own_half)
+
+
+def top_level(mix, q, g, gate, is_open, first, own, state, own_norm=None):
+    wide = sds((ROWS, HROWS))
+    args = [mix, q, g, gate, is_open, first, *own, state]
+    if own_norm is not None:
+        args.append(own_norm)
+    return call(
+        functools.partial(top_level_kernel, own_norm is None),
+        [sds((ROWS, HROWS if own_norm is None else FROWS), BF16), wide, wide, sds((HROWS, HD))],
+        *args, flops=4 * ROWS * HD * FROWS,
+        name="top_own" if own_norm is None else "top_other",
     )
 
 
 def gate_grads_kernel(
-    dsum_ref, same_ref, near_ref, p0, p1, p2, p3, p4, slope_ref, open_ref, s0, a1, a2, a3, a4, out
+    dsum_own, dsum_other, same_ref, near_ref, p0, p1, p2, p3, p4_own, p4_other, slope_ref,
+    open_ref, s0, a1, a2, a3, a4, out
 ):
     usable = usable_rows(flag_rows(s0, (a1, a2, a3, a4)))
     lane = lax.broadcasted_iota(jnp.int32, (ROWS, HD), 1)
     out[...] = jnp.zeros((ROWS, HD), F32)
 
-    def head(h, carry):
-        dsum = dsum_ref[:, cut(h)]
+    def step(n, h, own):
+        dsum = (dsum_own if own else dsum_other)[:, cut(n)]
         near = jnp.sum(dsum[STRETCH:] * near_ref[:, cut(h)], axis=1, keepdims=True)
         values = [
             jnp.sum(dsum * same_ref[:, cut(h)], axis=1, keepdims=True),
             rows(jnp.zeros((STRETCH, 1), F32), near),
         ]
-        for ref in (p0, p1, p2, p3, p4):
+        for ref in (p0, p1, p2, p3):
             values.append(jnp.sum(dsum * ref[:, cut(h)], axis=1, keepdims=True))
+        top = (p4_own if own else p4_other)[:, cut(n)]
+        values.append(jnp.sum(dsum * top, axis=1, keepdims=True))
         spread = out[...]
         for slot, value in enumerate(values):
             spread = jnp.where(lane == slot * HEADS + h, value, spread)
         out[...] = spread
-        return carry
-
-    lax.fori_loop(0, HEADS, head, 0, unroll=2)
+
+    per_head(step)
     factor = slope_ref[...]
     mask = open_ref[...]
     for b in range(BITS):
@@ -361,22 +371,23 @@
     out[...] = out[...] * factor
 
 
-def gate_grads(dsum, same, near, prods, slope, is_open, first, own):
-    return call(
-        gate_grads_kernel, sds((ROWS, HD)), dsum, same, near, *prods, slope, is_open, first, *own,
-        flops=14 * ROWS * FROWS, name="gate_grads",
+def gate_grads(dsums, same, near, prods, slope, is_open, first, own):
+    return call(
+        gate_grads_kernel, sds((ROWS, HD)), *dsums, same, near, *prods, slope, is_open, first,
+        *own, flops=14 * ROWS * FROWS, name="gate_grads",
     )
 
 
 def state_grads_kernel(
-    q_ref, dsum_ref, gate_ref, open_ref, s0, a1, a2, a3, d0, da1, da2, da3, do1, do2, do3
+    q_ref, dsum_own, dsum_other, gate_ref, open_ref, s0, a1, a2, a3, d0, da1, da2, da3, do1, do2,
+    do3
 ):
     usable = usable_rows(flag_rows(s0, (a1, a2, a3)))
     mask = open_ref[...]
 
     def step(n, h, own):
         cols = head_columns(gate_ref, h)
-        dsum = dsum_ref[:, cut(h)]
+        dsum = (dsum_own if own else dsum_other)[:, cut(n)]
         parts = [level_weight(cols, mask, usable[b], b) * dsum for b in range(4)]
         high, low = split(lanes(*parts))
         q = q_ref[:, cut(h)]
@@ -388,10 +399,10 @@
     per_head(step)
 
 
-def state_grads(q, dsum, gate, is_open, first, own):
+def state_grads(q, dsums, gate, is_open, first, own):
     half = sds((HROWS, HD))
     return call(
-        state_grads_kernel, [sds((FROWS, HD))] + [half] * 6, q, dsum, gate, is_open, first, *own,
+        state_grads_kernel, [sds((FROWS, HD))] + [half] * 6, q, *dsums, gate, is_open, first, *own,
         flops=16 * ROWS * HD * FROWS, name="state_grads",
     )
 
@@ -435,11 +446,12 @@
     return call(total_kernel, sds(arrays[0].shape), *arrays, flops=arrays[0].size, name=name)
 
 
-def local_kernel(
-    q_ref, k_ref, v_ref, dsum_ref, gate_ref, pair_ref, open_ref, s0, a1, a2, a3, a4, o1, o2, o3, o4,
-    gq_ref, gk_ref, gv_ref
-):
-    usable = usable_rows(flag_rows(s0, (a1, a2, a3, a4)))
+def local_kernel(own_half, *refs):
+    q_ref, k_ref, v_ref, dsum_ref, gate_ref, pair_ref, open_ref, s0 = refs[:8]
+    flags, levels = refs[8:12], refs[8:12] if own_half else refs[12:16]
+    gq_ref, gk_ref, gv_ref = refs[-3:]
+    own_grad = None if own_half else refs[16]
+    usable = usable_rows(flag_rows(s0, flags))
 
     def step(n, h, own):
         q, k, v = q_ref[:, cut(h)], k_ref[:, cut(h)], v_ref[:, cut(h)]
@@ -447,32 +459,37 @@
         mask = pair_ref[...]
         raw, left, g0, first = local_weights(q, k, cols, mask)
         wh, wl = split(by_columns(raw, left, g0))
-        dh, dm, dl = split3(dsum_ref[:, cut(h)])
+        dh, dm, dl = split3(dsum_ref[:, cut(n)])
         dots = dot(lanes(dh, dm, dl), lanes(v, v, v), NT)
         bh, bl = split(by_columns(dots * mask, left, g0))
         grad_q = dot(bh, k) + dot(bl, k)
-        gk_ref[:, cut(h)] = dot(bh, q, TN) + dot(bl, q, TN)
+        gk_ref[:, cut(n)] = dot(bh, q, TN) + dot(bl, q, TN)
         both = dot(wh, lanes(dh, dm), TN)
-        gv_ref[:, cut(h)] = both[:, :HD] + both[:, HD:] + dot(wl, dh, TN)
+        gv_ref[:, cut(n)] = both[:, :HD] + both[:, HD:] + dot(wl, dh, TN)
 
         open_mask = open_ref[...]
-        refs = (a1, a2, a3, a4) if own else (o1, o2, o3, o4)
-        states = [s0[cut(h), :]] + [r[cut(n), :] for r in refs]
+        states = [s0[cut(h), :]] + [r[cut(n), :] for r in levels]
         sh, sl = split(rows(*states))
         back_all = dot(lanes(dh, dh, dm), lanes(sh, sl, sh), NT)
         for b in range(BITS):
             part = back_all[:, b * HD : (b + 1) * HD]
             grad_q = grad_q + level_weight(cols, open_mask, usable[b], b) * part
-        gq_ref[:, cut(h)] = grad_q.astype(BF16)
-
-    per_head(step)
-
-
-def local_grads(q, k, v, dsum, gate, pair, is_open, first, own, other):
-    return call(
-        local_kernel, [sds((ROWS, FROWS), BF16), sds((ROWS, FROWS)), sds((ROWS, FROWS))],
-        q, k, v, dsum, gate, pair, is_open, first, *own, *other, flops=60 * ROWS * HD * FROWS,
-        name="local_grads",
+        gq_ref[:, cut(n if own_half else h)] = grad_q.astype(BF16)
+        if not own_half:
+            gq_ref[:, cut(HALF * core() + n)] = own_grad[:, cut(n)]
+
+    per_head(step, own=own_half, other=not own_half)
+
+
+def local_grads(q, k, v, dsum, gate, pair, is_open, first, own, other=(), own_grad=None):
+    args = [q, k, v, dsum, gate, pair, is_open, first, *own, *other]
+    if other:
+        args.append(own_grad)
+    half = sds((ROWS, HROWS))
+    return call(
+        functools.partial(local_kernel, not other),
+        [sds((ROWS, FROWS if other else HROWS), BF16), half, half], *args,
+        flops=30 * ROWS * HD * FROWS, name="local_other" if other else "local_own",
     )
 
 
@@ -486,7 +503,7 @@
     return call(final_kernel, sds((FROWS, HD)), own, other, flops=FROWS * HD, name="final")
 
 
-def ends_kernel(k_ref, v_ref, gk_ref, gv_ref, keys_ref, wa, wo, d0, s0, ok_ref, ov_ref):
+def ends_kernel(k_ref, v_ref, gk_own, gv_own, gk_other, gv_other, keys_ref, wa, wo, d0, s0, ok_ref, ov_ref):
     lower = core() == 0
     flag = s0[FROWS : FROWS + 1, :]
     keep = jnp.where(lower, 1.0 - flag, jnp.ones_like(flag))
@@ -498,16 +515,17 @@
         k, v = k_ref[:, cut(h)], v_ref[:, cut(h)]
         by_value = dot(lanes(v, v), lanes(high, low), NT)
         by_key = dot(lanes(k, k), rows(high, low))
-        ok_ref[:, cut(h)] = (gk_ref[:, cut(h)] + mask * by_value).astype(BF16)
-        ov_ref[:, cut(h)] = (gv_ref[:, cut(h)] + mask * by_key).astype(BF16)
+        gk_ref, gv_ref = (gk_own, gv_own) if own else (gk_other, gv_other)
+        ok_ref[:, cut(h)] = (gk_ref[:, cut(n)] + mask * by_value).astype(BF16)
+        ov_ref[:, cut(h)] = (gv_ref[:, cut(n)] + mask * by_key).astype(BF16)
 
     per_head(step)
 
 
-def ends(k, v, gk, gv, keys, w_own, w_other, d0, first):
-    return call(
-        ends_kernel, [sds((ROWS, FROWS), BF16)] * 2, k, v, gk, gv, keys, w_own, w_other, d0, first,
-        flops=8 * ROWS * HD * FROWS, name="ends",
+def ends(k, v, own, other, keys, w_own, w_other, d0, first):
+    return call(
+        ends_kernel, [sds((ROWS, FROWS), BF16)] * 2, k, v, *own, *other, keys, w_own,
+        w_other, d0, first, flops=8 * ROWS * HD * FROWS, name="ends",
     )
 
 
@@ -520,7 +538,9 @@
         x = x_ref[:, cut(p)]
         grad = dot(rows(x, x), stacked, TN)
         upper, lower = grad[:SHARE], grad[SHARE:]
-        at = pl.ds(pl.multiple_of(p * SHARE, SHARE), SHARE)
+        chip_in_row = lax.rem(p, 4)
+        turned = jnp.where(chip_in_row == 0, 0, lax.rem(chip_in_row, 3) + 1)
+        at = pl.ds(pl.multiple_of((p - chip_in_row + turned) * SHARE, SHARE), SHARE)
         own_ref[at, :] = jnp.where(first, upper, lower)
         other_ref[at, :] = jnp.where(first, lower, upper)
         return carry
@@ -545,11 +565,14 @@
     return kernel
 
 
-def halve(a, b, bit):
+def outer_x():
+    return lax.rem(bit_of(1) + bit_of(2), 2)
+
+
+def halve(a, b, side_of, name):
     length = a.shape[0] // 2
     return call(
-        halve_kernel(lambda: bit_of(bit), length), [sds((length, HD))] * 2, a, b, flops=a.size,
-        name=f"halve{bit}",
+        halve_kernel(side_of, length), [sds((length, HD))] * 2, a, b, flops=a.size, name=name
     )
 
 
@@ -604,7 +627,10 @@
         if b < BITS - 1:
             blocks[b + 1] = join(blocks[b], got, b)
 
-    normed, dsum, prod4, da4, do4 = top_level(mix, q, g, gate, is_open, first, own, other[3])
+    own_norm, dsum_own, prod_own, da4 = top_level(mix, q, g, gate, is_open, first, own, own[3])
+    normed, dsum_other, prod_other, do4 = top_level(
+        mix, q, g, gate, is_open, first, own, other[3], own_norm
+    )
     d_own, d_other = [None, None, None, da4], [None, None, None, do4]
     ws = [fg]
     for b in reversed(range(1, BITS)):
@@ -612,42 +638,52 @@
         to_partner, kept = back(b, ws, d_own[b - 1], got, blocks[b], own[b - 1])
         moved = swap(to_partner, b, f"down{b}")
         if b == 4:
-            dlog = gate_grads(dsum, same, near, [*prods, prod4], slope, is_open, first, own)
+            d0, *rest = state_grads(
+                q, (hold(dsum_own, kept), dsum_other), gate, is_open, first, own[:3]
+            )
+            d_own[:3], d_other[:3] = rest[:3], rest[3:]
+            dlog = gate_grads(
+                (hold(dsum_own, d0), dsum_other), same, near, [*prods, prod_own, prod_other],
+                slope, is_open, first, own,
+            )
             share, send = project(x, dlog)
             send = swap(send, 0, "share")
-            d0, *rest = state_grads(q, hold(dsum, share), gate, is_open, first, own[:3])
-            d_own[:3], d_other[:3] = rest[:3], rest[3:]
-            moved = hold(moved, d0)
+            moved = hold(moved, share)
         elif b == 3:
-            share, send = halve(share, send, 4)
-            send = swap(send, 4, "share4")
-            grad_q, gk, gv = local_grads(
-                q, k, v, hold(dsum, share), gate, pair, is_open, first, own, other
-            )
-            moved = hold(moved, gk)
-        elif b == 2:
-            blocks[5] = join(blocks[4], own[3], 4)
+            share, send = halve(share, send, lambda: bit_of(4), "halve_z2")
+            send = swap(send, 4, "share_z2")
+            part = local_grads(q, k, v, hold(dsum_own, share), gate, pair, is_open, first, own)
+            blocks[5] = join(hold(blocks[4], part[1]), own[3], 4)
             fin_other = swap(blocks[5], 0, "fin")
             d0_got = lax.ppermute(d0, "seq", [(i + 1, i) for i in range(0, 32, 2)])
-            share, send = halve(share, send, 3)
-            send = swap(send, 3, "share3")
-            share, send = halve(share, send, 2)
-            moved = hold(moved, share, blocks[5])
+            share, send = halve(
+                share, hold(send, blocks[5]), lambda: bit_of(3), "halve_z1"
+            )
+            send = swap(send, 3, "share_z1")
+            moved = hold(moved, share)
+        elif b == 2:
+            share, send = halve(share, send, outer_x, "halve_x1")
+            send = swap(send, 1, "share_x1")
+            rest_part = local_grads(
+                q, k, v, hold(dsum_other, share), gate, pair, is_open, first, own, other, part[0]
+            )
+            grad_q = rest_part[0]
+            row = total([share, hold(send, grad_q)], "row")
+            moved = hold(moved, row)
         else:
-            send = swap(send, 2, "share2")
-            fin = final(blocks[5], fin_other)
-            share, send = halve(share, send, 1)
-            send = swap(send, 1, "share1")
-            moved = hold(moved, share, fin)
+            row = total([row, swap_y(row, 3, "share_y2")], "row2")
+            fin = final(blocks[5], hold(fin_other, row))
+            share, send = halve(
+                row, hold(swap_y(row, 1, "share_y1"), fin), lambda: bit_of(2), "halve_x2"
+            )
+            send = swap(send, 2, "share_x2")
+            moved = hold(moved, share)
         ws = [kept, moved]
     w_own = total(ws, "w_chip")
     w_other = swap(w_own, 0, "half0")
-
-    row = total([share, send], "row")
-    row = total([row, swap_y(row, 3, "share_y2")], "row2")
-    grad_level = widen(row, swap_y(row, 1, "share_y1"))
-
-    grad_k, grad_v = ends(k, v, gk, gv, keys, w_own, w_other, d0_got, first)
+    grad_level = widen(share, send)
+
+    grad_k, grad_v = ends(k, v, part[1:], rest_part[1:], keys, w_own, w_other, d0_got, first)
     flat = (1, ROWS, FROWS)
     return (
         normed.reshape(flat),

time: 136 us -> 129 us (0.949)
  waiting for transfers between devices: 56.9 us -> 52.8 us
  starting transfers between devices: 30.9 us -> 27.3 us
    ppermute x24, waiting for transfers between devices: 51.2 us -> 47 us  [swap(): return lax.ppermute(value, 'seq', [(i, i ^ FLIP[bit]) for i in range(32)])]
    ppermute x24, starting transfers between devices: 26.2 us -> 22.4 us  [swap(): return lax.ppermute(value, 'seq', [(i, i ^ FLIP[bit]) for i in range(32)])]
    pallas_call x28 -> x30, Pallas kernels: 44 us -> 44.3 us  [call(): pl.pallas_call(kernel, in_specs=in_specs, out_specs=out_specs if isinstan...]
  transfers between devices with their start and end apart: 27 -> 27, of which waited for: 14 -> 13; matrix products, arithmetic and copies ran while one was open for 0% -> 0% of each run, Pallas kernels for 24% -> 28%
where the time goes in v1:
time: 129 us; the launch traced here: 128 us
  waiting for transfers between devices  52.8 us (41%)
  Pallas kernels  44.3 us (34%)
  starting transfers between devices  27.3 us (21%)
  local copies, waits for them, and re-layouts  2.95 us (2%)
    ppermute x24, waiting for transfers between devices, swap(): return lax.ppermute(value, 'seq', [(i, i ^ FLIP[bit]) for i in range(32)])  47 us
    pallas_call x30, Pallas kernels, call(): pl.pallas_call(kernel, in_specs=in_specs, out_specs=out_specs if isinstan...  44.3 us
    ppermute x24, starting transfers between devices, swap(): return lax.ppermute(value, 'seq', [(i, i ^ FLIP[bit]) for i in range(32)])  22.4 us
    ppermute x2, waiting for transfers between devices, swap_y(): return lax.ppermute(value, 'dp', [(i, i ^ flip) for i in range(4)])  5.78 us
    ppermute x2, starting transfers between devices, swap_y(): return lax.ppermute(value, 'dp', [(i, i ^ flip) for i in range(4)])  3.61 us
    unnamed x20, local copies, waits for them, and re-layouts  2.95 us
  transfers between devices with their start and end apart: 27, of which 13 were waited for; matrix products, arithmetic and copies ran while one was open for 0% of the time, Pallas kernels for 28%

profile of v1, /device:TPU:0, one launch (start us, length us, event | category | flops | bytes accessed | tf_op | source)
XLA Modules:
  0.0 128.3 jit_solution(5871831070849358070)
XLA Ops:
  3.6 1.6 %tails.1 = (f32[1544,128]{1,0:T(8,128)S(1)}, f32[256,128]{1,0:T(8,128)S(1)}, f32[256,128]{1,0:T(8,128)S(1)}, f32[256,256]{1,0:T(8,128)S(1)}) custom-call(s32[1,2]{1,0:T(1,128)S(1)} %copy-done.9, bf16[256,1536]{1,0:T(8,128)(2,1)S(1)} %bitcast.19, bf16[256,1536]{1,0:T(8,128)(2,1)S(1)} %bitcast.24), custom_call_target="tpu_custom_call" | custom-call | flops 100663296 | bytes 2887688 | tf_op jit(solution)/shard_map/tails/tails/pallas_call | solution.py:87
  5.3 2.3 %collective-permute-done.b_ref.s0.refs_5_.refs_7_ = f32[1544,128]{1,0:T(8,128)S(1)} collective-permute-done((f32[1544,128]{1,0:T(8,128)S(1)}, f32[1544,128]{1,0:T(8,128)S(1)}, u32[]{:S(2)}, u32[]{:S(2)}) %collective-permute-start) | collective-permute-done | bytes 790560 | tf_op jit(solution)/shard_map/turn0/ppermute | solution.py:593
  7.7 1.7 %collective-permute-start.1 = (f32[776,128]{1,0:T(8,128)S(1)}, f32[776,128]{1,0:T(8,128)S(1)}, u32[]{:S(2)}, u32[]{:S(2)}) collective-permute-start(f32[776,128]{1,0:T(8,128)S(1)} %join0.1.a_ref.refs_4_), channel_id=1, source_target_pairs={{0,8},{4,12},{8,0},{12,4},{16,24},{20,28},{24,16},{28,20},{32,40},... | collective-permute-start | bytes 1191944 | tf_op jit(solution)/shard_map/up1/ppermute | solution.py:593
  9.8 9.2 %collective-permute-done.1.b_ref.a1.refs_6_.refs_8_.refs_5_ = f32[776,128]{1,0:T(8,128)S(1)} collective-permute-done((f32[776,128]{1,0:T(8,128)S(1)}, f32[776,128]{1,0:T(8,128)S(1)}, u32[]{:S(2)}, u32[]{:S(2)}) %collective-permute-start.1) | collective-permute-done | bytes 397344 | tf_op jit(solution)/shard_map/up1/ppermute | solution.py:593
  19.1 2.9 %collective-permute-start.2 = (f32[776,128]{1,0:T(8,128)S(1)}, f32[776,128]{1,0:T(8,128)S(1)}, u32[]{:S(2)}, u32[]{:S(2)}) collective-permute-start(f32[776,128]{1,0:T(8,128)S(1)} %join1.1.a_ref.refs_4_), channel_id=1, source_target_pairs={{0,24},{4,28},{8,16},{12,20},{16,8},{20,12},{24,0},{28,4},{32,56},... | collective-permute-start | bytes 1191944 | tf_op jit(solution)/shard_map/up2/ppermute | solution.py:593
  22.0 3.8 %intra.1 = (f32[256,1536]{1,0:T(8,128)S(1)}, f32[128,1536]{1,0:T(8,128)S(1)}) custom-call(bf16[256,1536]{1,0:T(8,128)(2,1)S(1)} %bitcast.12, bf16[256,1536]{1,0:T(8,128)(2,1)S(1)} %bitcast.20, bf16[256,1536]{1,0:T(8,128)(2,1)S(1)} %bitcast.25, f32[256,256]{1,0:T(8,128)S(1)} %get-tuple-element.76.pair_ref.refs_5_), custom_call_target="tpu_custom_call" | custom-call | flops 603979776 | bytes 4980736 | tf_op jit(solution)/shard_map/intra/intra/pallas_call | solution.py:87
  25.8 4.9 %collective-permute-done.2.b_ref.a2.refs_7_.refs_9_.refs_5_ = f32[776,128]{1,0:T(8,128)S(1)} collective-permute-done((f32[776,128]{1,0:T(8,128)S(1)}, f32[776,128]{1,0:T(8,128)S(1)}, u32[]{:S(2)}, u32[]{:S(2)}) %collective-permute-start.2) | collective-permute-done | bytes 397344 | tf_op jit(solution)/shard_map/up2/ppermute | solution.py:593
  30.8 2.1 %collective-permute-start.3 = (f32[776,128]{1,0:T(8,128)S(1)}, f32[776,128]{1,0:T(8,128)S(1)}, u32[]{:S(2)}, u32[]{:S(2)}) collective-permute-start(f32[776,128]{1,0:T(8,128)S(1)} %join2.1.a_ref.refs_4_), channel_id=1, source_target_pairs={{0,32},{4,36},{8,40},{12,44},{16,48},{20,52},{24,56},{28,60},{32,0... | collective-permute-start | bytes 1191944 | tf_op jit(solution)/shard_map/up3/ppermute | solution.py:593
  33.4 7.3 %collective-permute-done.3.a3.b_ref.refs_8_.refs_10_.refs_5_ = f32[776,128]{1,0:T(8,128)S(1)} collective-permute-done((f32[776,128]{1,0:T(8,128)S(1)}, f32[776,128]{1,0:T(8,128)S(1)}, u32[]{:S(2)}, u32[]{:S(2)}) %collective-permute-start.3) | collective-permute-done | bytes 397344 | tf_op jit(solution)/shard_map/up3/ppermute | solution.py:593
  40.8 3.9 %collective-permute-start.7 = (f32[776,128]{1,0:T(8,128)S(1)}, f32[776,128]{1,0:T(8,128)S(1)}, u32[]{:S(2)}, u32[]{:S(2)}) collective-permute-start(f32[776,128]{1,0:T(8,128)S(1)} %join3.1.refs_3_.a_ref), channel_id=1, source_target_pairs={{0,96},{4,100},{8,104},{12,108},{16,112},{20,116},{24,120},{28,124... | collective-permute-start | bytes 1191944 | tf_op jit(solution)/shard_map/up4/ppermute | solution.py:593
  44.7 5.4 %low_levels.1 = (f32[256,1536]{1,0:T(8,128)S(1)}, f32[256,1536]{1,0:T(8,128)S(1)}, f32[256,1536]{1,0:T(8,128)S(1)}, f32[256,1536]{1,0:T(8,128)S(1)}, f32[256,1536]{1,0:T(8,128)S(1)}) custom-call(f32[256,1536]{1,0:T(8,128)S(1)} %get-tuple-element.77.same_ref, f32[128,1536]{1,0:T(8,128)S(1)} %get-tuple-element.78.near_ref, bf16[256,1536]{1,0:T(8,128)(2,1)S(1)} %bitcast.13, ...), custom_call_target="tpu_custom_call" | custom-call | flops 805306368 | bytes 14446592 | tf_op jit(solution)/shard_map/low_levels/low_levels/pallas_call | solution.py:87
  50.1 4.4 %collective-permute-done.7.refs_9_.refs_10_.refs_4_.a4.refs_11_.b_ref = f32[776,128]{1,0:T(8,128)S(1)} collective-permute-done((f32[776,128]{1,0:T(8,128)S(1)}, f32[776,128]{1,0:T(8,128)S(1)}, u32[]{:S(2)}, u32[]{:S(2)}) %collective-permute-start.7) | collective-permute-done | bytes 397344 | tf_op jit(solution)/shard_map/up4/ppermute | solution.py:593
  54.6 3.0 %top_own.1 = (bf16[256,768]{1,0:T(8,128)(2,1)S(1)}, f32[256,768]{1,0:T(8,128)S(1)}, f32[256,768]{1,0:T(8,128)S(1)}, f32[768,128]{1,0:T(8,128)S(1)}) custom-call(f32[256,1536]{1,0:T(8,128)S(1)} %get-tuple-element.84.refs_0_, bf16[256,1536]{1,0:T(8,128)(2,1)S(1)} %bitcast.14, bf16[256,1536]{1,0:T(8,128)(2,1)S(1)} %bitcast.31, ...), custom_call_target="tpu_custom_call" | custom-call | flops 201326592 | bytes 8544256 | tf_op jit(solution)/shard_map/top_own/top_own/pallas_call | solution.py:87
  57.6 3.7 %top_other.1 = (bf16[256,1536]{1,0:T(8,128)(2,1)}, f32[256,768]{1,0:T(8,128)S(1)}, f32[256,768]{1,0:T(8,128)S(1)}, f32[768,128]{1,0:T(8,128)S(1)}) custom-call(f32[256,1536]{1,0:T(8,128)S(1)} %get-tuple-element.84.refs_0_, bf16[256,1536]{1,0:T(8,128)(2,1)S(1)} %bitcast.15, bf16[256,1536]{1,0:T(8,128)(2,1)S(1)} %bitcast.32, ...), custom_call_target="tpu_custom_call" | custom-call | flops 201326592 | bytes 9330688 | tf_op jit(solution)/shard_map/top_other/top_other/pallas_call | solution.py:87
  61.8 1.3 %collective-permute-done.9.refs_2_ = f32[768,128]{1,0:T(8,128)S(1)} collective-permute-done((f32[768,128]{1,0:T(8,128)S(1)}, f32[768,128]{1,0:T(8,128)S(1)}, u32[]{:S(2)}, u32[]{:S(2)}) %collective-permute-start.9) | collective-permute-done | bytes 393248 | tf_op jit(solution)/shard_map/half4/ppermute | solution.py:593
  63.3 3.0 %collective-permute-start.13 = (f32[768,128]{1,0:T(8,128)S(1)}, f32[768,128]{1,0:T(8,128)S(1)}, u32[]{:S(2)}, u32[]{:S(2)}) collective-permute-start(f32[768,128]{1,0:T(8,128)S(1)} %get-tuple-element.121), channel_id=1, source_target_pairs={{0,96},{4,100},{8,104},{12,108},{16,112},{20,116},{24,120},{28,124... | collective-permute-start | bytes 1179656 | tf_op jit(solution)/shard_map/down4/ppermute | solution.py:593
  66.3 4.8 %state_grads.1 = (f32[1536,128]{1,0:T(8,128)S(1)}, f32[768,128]{1,0:T(8,128)S(1)}, f32[768,128]{1,0:T(8,128)S(1)}, f32[768,128]{1,0:T(8,128)S(1)}, f32[768,128]{...) custom-call(bf16[256,1536]{1,0:T(8,128)(2,1)S(1)} %bitcast.16, ...), custom_call_target="tpu_custom_call" | custom-call | flops 805306368 | bytes 7749632 | tf_op jit(solution)/shard_map/state_grads/state_grads/pallas_call | solution.py:87
  71.2 3.7 %gate_grads.1.d_ref = f32[256,128]{1,0:T(8,128)S(1)} custom-call(f32[256,768]{1,0:T(8,128)S(1)} %get-tuple-element.107.dsum_own.refs_3_, f32[256,768]{1,0:T(8,128)S(1)} %get-tuple-element.114.dsum_other.refs_3_, f32[256,1536]{1,0:T(8,128)S(1)} %get-tuple-element.77.same_ref, f32[128,1536]{1,0:T(8,128)S(1)} %get-tuple-element.78.near_ref, ...), custom_call_target="tpu_custom_call" | custom-call | flops 5505024 | bytes 14569472 | tf_op jit(solution)/shard_map/gate_grads/gate_grads/pallas_call | solution.py:87
  74.9 2.1 %project.1 = (f32[1024,128]{1,0:T(8,128)S(1)}, f32[1024,128]{1,0:T(8,128)S(1)}) custom-call(bf16[256,2048]{1,0:T(8,128)(2,1)S(1)} %bitcast.30, f32[256,128]{1,0:T(8,128)S(1)} %gate_grads.1.d_ref), custom_call_target="tpu_custom_call" | custom-call | flops 268435456 | bytes 2228224 | tf_op jit(solution)/shard_map/project/project/pallas_call | solution.py:87
  77.6 2.0 %collective-permute-done.14.refs_3_ = f32[768,128]{1,0:T(8,128)S(1)} collective-permute-done((f32[768,128]{1,0:T(8,128)S(1)}, f32[768,128]{1,0:T(8,128)S(1)}, u32[]{:S(2)}, u32[]{:S(2)}) %collective-permute-start.14) | collective-permute-done | bytes 393248 | tf_op jit(solution)/shard_map/half3/ppermute | solution.py:593
  80.6 4.6 %local_own.1 = (bf16[256,768]{1,0:T(8,128)(2,1)S(1)}, f32[256,768]{1,0:T(8,128)S(1)}, f32[256,768]{1,0:T(8,128)S(1)}) custom-call(bf16[256,1536]{1,0:T(8,128)(2,1)S(1)} %bitcast.17, bf16[256,1536]{1,0:T(8,128)(2,1)S(1)} %bitcast.21, bf16[256,1536]{1,0:T(8,128)(2,1)S(1)} %bitcast.26, f32[256,768]{1,0:T(8,128)S(1)} %get-tuple-element.107.dsum_own.refs_3_, ...), custom_call_target="tpu_custom_call" | custom-call | flops 1509949440 | bytes 8015872 | tf_op jit(solution)/shard_map/local_own/local_own/pallas_call | solution.py:87
  85.3 4.8 %collective-permute-done.11.b_ref = f32[512,128]{1,0:T(8,128)S(1)} collective-permute-done((f32[512,128]{1,0:T(8,128)S(1)}, f32[512,128]{1,0:T(8,128)S(1)}, u32[]{:S(2)}, u32[]{:S(2)}) %collective-permute-start.11) | collective-permute-done | bytes 262176 | tf_op jit(solution)/shard_map/share_z2/ppermute | solution.py:593
  91.0 2.8 %collective-permute-start.17 = (f32[768,128]{1,0:T(8,128)S(1)}, f32[768,128]{1,0:T(8,128)S(1)}, u32[]{:S(2)}, u32[]{:S(2)}) collective-permute-start(f32[768,128]{1,0:T(8,128)S(1)} %get-tuple-element.131), channel_id=1, source_target_pairs={{0,24},{4,28},{8,16},{12,20},{16,8},{20,12},{24,0},{28,4},{32,56},... | collective-permute-start | bytes 1179656 | tf_op jit(solution)/shard_map/down2/ppermute | solution.py:593
  94.4 5.4 %collective-permute-done.12.b_ref = f32[256,128]{1,0:T(8,128)S(1)} collective-permute-done((f32[256,128]{1,0:T(8,128)S(1)}, f32[256,128]{1,0:T(8,128)S(1)}, u32[]{:S(2)}, u32[]{:S(2)}) %collective-permute-start.12) | collective-permute-done | bytes 131104 | tf_op jit(solution)/shard_map/share_z1/ppermute | solution.py:593
  99.9 5.5 %local_other.1 = (bf16[256,1536]{1,0:T(8,128)(2,1)}, f32[256,768]{1,0:T(8,128)S(1)}, f32[256,768]{1,0:T(8,128)S(1)}) custom-call(bf16[256,1536]{1,0:T(8,128)(2,1)S(1)} %bitcast.18, bf16[256,1536]{1,0:T(8,128)(2,1)S(1)} %bitcast.22, bf16[256,1536]{1,0:T(8,128)(2,1)S(1)} %bitcast.27, f32[256,768]{1,0:T(8,128)S(1)} %get-tuple-element.114.dsum_other.refs_3_, ...), custom_call_target="tpu_custom_call" | custom-call | flops 1509949440 | bytes 10391552 | tf_op jit(solution)/shard_map/local_other/local_other/pallas_call | solution.py:87
  105.6 2.1 %collective-permute-start.20 = (f32[768,128]{1,0:T(8,128)S(1)}, f32[768,128]{1,0:T(8,128)S(1)}, u32[]{:S(2)}, u32[]{:S(2)}) collective-permute-start(f32[768,128]{1,0:T(8,128)S(1)} %get-tuple-element.138), channel_id=1, source_target_pairs={{0,8},{4,12},{8,0},{12,4},{16,24},{20,28},{24,16},{28,20},{32,40},... | collective-permute-start | bytes 1179656 | tf_op jit(solution)/shard_map/down1/ppermute | solution.py:593
  107.7 1.3 collective-permute-start.25
  109.0 3.1 %collective-permute-start.21 = (f32[128,128]{1,0:T(8,128)S(1)}, f32[128,128]{1,0:T(8,128)S(1)}, u32[]{:S(2)}, u32[]{:S(2)}) collective-permute-start(f32[128,128]{1,0:T(8,128)S(1)} %row.1.refs_0_), channel_id=1, source_target_pairs={{0,3},{1,2},{2,1},{3,0},{4,7},{5,6},{6,5},{7,4},{8,11},{9,10},{10,... | collective-permute-start | bytes 196616 | tf_op jit(solution)/shard_map/share_y2/ppermute | solution.py:598
  112.1 2.9 %collective-permute-done.21.refs_1_ = f32[128,128]{1,0:T(8,128)S(1)} collective-permute-done((f32[128,128]{1,0:T(8,128)S(1)}, f32[128,128]{1,0:T(8,128)S(1)}, u32[]{:S(2)}, u32[]{:S(2)}) %collective-permute-start.21) | collective-permute-done | bytes 65568 | tf_op jit(solution)/shard_map/share_y2/ppermute | solution.py:598
  116.4 2.9 %collective-permute-done.22.b_ref = f32[128,128]{1,0:T(8,128)S(1)} collective-permute-done((f32[128,128]{1,0:T(8,128)S(1)}, f32[128,128]{1,0:T(8,128)S(1)}, u32[]{:S(2)}, u32[]{:S(2)}) %collective-permute-start.22) | collective-permute-done | bytes 65568 | tf_op jit(solution)/shard_map/share_y1/ppermute | solution.py:598
  120.1 4.6 %collective-permute-done.26.b_ref = f32[64,128]{1,0:T(8,128)S(1)} collective-permute-done((f32[64,128]{1,0:T(8,128)S(1)}, f32[64,128]{1,0:T(8,128)S(1)}, u32[]{:S(2)}, u32[]{:S(2)}) %collective-permute-start.26) | collective-permute-done | bytes 32800 | tf_op jit(solution)/shard_map/share_x2/ppermute | solution.py:593
  125.3 2.9 %ends.1 = (bf16[256,1536]{1,0:T(8,128)(2,1)}, bf16[256,1536]{1,0:T(8,128)(2,1)}) custom-call(bf16[256,1536]{1,0:T(8,128)(2,1)S(1)} %bitcast.23, bf16[256,1536]{1,0:T(8,128)(2,1)S(1)} %bitcast.28, f32[256,768]{1,0:T(8,128)S(1)} %get-tuple-element.108.gk_own, f32[256,768]{1,0:T(8,128)S(1)} %get-tuple-element.117.gv_own, ...), custom_call_target="tpu_custom_call" | custom-call | flops 402653184 | bytes 8785920 | tf_op jit(solution)/shard_map/ends/ends/pallas_call | solution.py:87
  (72 shorter events, 11.1 us)
Async XLA Ops:
  3.6 5.8 %copy-start.7 = (bf16[2048,144]{0,1:T(8,128)(2,1)S(1)}, bf16[2048,144]{0,1:T(8,128)(2,1)}, u32[]{:S(2)}) copy-start(bf16[2048,144]{0,1:T(8,128)(2,1)} %param.12) | copy-start | bytes 1769476
  5.2 2.4 %collective-permute-start = (f32[1544,128]{1,0:T(8,128)S(1)}, f32[1544,128]{1,0:T(8,128)S(1)}, u32[]{:S(2)}, u32[]{:S(2)}) collective-permute-start(f32[1544,128]{1,0:T(8,128)S(1)} %get-tuple-element.81.a_ref), channel_id=1, source_target_pairs={{0,4},{4,0},{8,12},{12,8},{16,20},{20,16},{24,28},{28,24},{32,36},... | collective-permute-start | bytes 2371592 | tf_op jit(solution)/shard_map/turn0/ppermute | solution.py:593
  7.6 14.4 %copy-start = (bf16[1,256,1536]{2,1,0:T(8,128)(2,1)S(1)}, bf16[1,256,1536]{2,1,0:T(8,128)(2,1)}, u32[]{:S(2)}) copy-start(bf16[1,256,1536]{2,1,0:T(8,128)(2,1)} %param.8) | copy-start | bytes 2359300
  7.7 14.4 %copy-start.2 = (bf16[1,256,1536]{2,1,0:T(8,128)(2,1)S(1)}, bf16[1,256,1536]{2,1,0:T(8,128)(2,1)}, u32[]{:S(2)}) copy-start(bf16[1,256,1536]{2,1,0:T(8,128)(2,1)} %param.9) | copy-start | bytes 2359300
  7.7 14.3 %copy-start.4 = (bf16[1,256,1536]{2,1,0:T(8,128)(2,1)S(1)}, bf16[1,256,1536]{2,1,0:T(8,128)(2,1)}, u32[]{:S(2)}) copy-start(bf16[1,256,1536]{2,1,0:T(8,128)(2,1)} %param.10) | copy-start | bytes 2359300
  7.7 11.3 %collective-permute-start.1 = (f32[776,128]{1,0:T(8,128)S(1)}, f32[776,128]{1,0:T(8,128)S(1)}, u32[]{:S(2)}, u32[]{:S(2)}) collective-permute-start(f32[776,128]{1,0:T(8,128)S(1)} %join0.1.a_ref.refs_4_), channel_id=1, source_target_pairs={{0,8},{4,12},{8,0},{12,4},{16,24},{20,28},{24,16},{28,20},{32,40},... | collective-permute-start | bytes 1191944 | tf_op jit(solution)/shard_map/up1/ppermute | solution.py:593
  19.1 11.7 %collective-permute-start.2 = (f32[776,128]{1,0:T(8,128)S(1)}, f32[776,128]{1,0:T(8,128)S(1)}, u32[]{:S(2)}, u32[]{:S(2)}) collective-permute-start(f32[776,128]{1,0:T(8,128)S(1)} %join1.1.a_ref.refs_4_), channel_id=1, source_target_pairs={{0,24},{4,28},{8,16},{12,20},{16,8},{20,12},{24,0},{28,4},{32,56},... | collective-permute-start | bytes 1191944 | tf_op jit(solution)/shard_map/up2/ppermute | solution.py:593
  30.8 9.9 %collective-permute-start.3 = (f32[776,128]{1,0:T(8,128)S(1)}, f32[776,128]{1,0:T(8,128)S(1)}, u32[]{:S(2)}, u32[]{:S(2)}) collective-permute-start(f32[776,128]{1,0:T(8,128)S(1)} %join2.1.a_ref.refs_4_), channel_id=1, source_target_pairs={{0,32},{4,36},{8,40},{12,44},{16,48},{20,52},{24,56},{28,60},{32,0... | collective-permute-start | bytes 1191944 | tf_op jit(solution)/shard_map/up3/ppermute | solution.py:593
  32.9 11.8 %collective-permute-start.4 = (f32[776,128]{1,0:T(8,128)S(1)}, f32[776,128]{1,0:T(8,128)S(1)}, u32[]{:S(2)}, u32[]{:S(2)}) collective-permute-start(f32[776,128]{1,0:T(8,128)S(1)} %collective-permute-done.1.b_ref.a1.refs_6_.refs_8_.refs_5_), channel_id=1, source_target_pairs={{0,4},{4,0},{8,12},{12,8},{16,20},{20,16},{24,28},{28,24},{32,36},... | collective-permute-start | bytes 1191944 | tf_op jit(solution)/shard_map/turn1/ppermute | solution.py:593
  32.9 11.8 %collective-permute-start.5 = (f32[776,128]{1,0:T(8,128)S(1)}, f32[776,128]{1,0:T(8,128)S(1)}, u32[]{:S(2)}, u32[]{:S(2)}) collective-permute-start(f32[776,128]{1,0:T(8,128)S(1)} %collective-permute-done.2.b_ref.a2.refs_7_.refs_9_.refs_5_), channel_id=1, source_target_pairs={{0,4},{4,0},{8,12},{12,8},{16,20},{20,16},{24,28},{28,24},{32,36},... | collective-permute-start | bytes 1191944 | tf_op jit(solution)/shard_map/turn2/ppermute | solution.py:593
  40.7 4.0 %collective-permute-start.6 = (f32[776,128]{1,0:T(8,128)S(1)}, f32[776,128]{1,0:T(8,128)S(1)}, u32[]{:S(2)}, u32[]{:S(2)}) collective-permute-start(f32[776,128]{1,0:T(8,128)S(1)} %collective-permute-done.3.a3.b_ref.refs_8_.refs_10_.refs_5_), channel_id=1, source_target_pairs={{0,4},{4,0},{8,12},{12,8},{16,20},{20,16},{24,28},{28,24},{32,36},... | collective-permute-start | bytes 1191944 | tf_op jit(solution)/shard_map/turn3/ppermute | solution.py:593
  40.8 13.8 %collective-permute-start.7 = (f32[776,128]{1,0:T(8,128)S(1)}, f32[776,128]{1,0:T(8,128)S(1)}, u32[]{:S(2)}, u32[]{:S(2)}) collective-permute-start(f32[776,128]{1,0:T(8,128)S(1)} %join3.1.refs_3_.a_ref), channel_id=1, source_target_pairs={{0,96},{4,100},{8,104},{12,108},{16,112},{20,116},{24,120},{28,124... | collective-permute-start | bytes 1191944 | tf_op jit(solution)/shard_map/up4/ppermute | solution.py:593
  44.7 9.9 %copy-start.6 = (bf16[1,256,1536]{2,1,0:T(8,128)(2,1)S(1)}, bf16[1,256,1536]{2,1,0:T(8,128)(2,1)}, u32[]{:S(2)}) copy-start(bf16[1,256,1536]{2,1,0:T(8,128)(2,1)} %param.14) | copy-start | bytes 2359300
  54.6 3.0 %collective-permute-start.8 = (f32[776,128]{1,0:T(8,128)S(1)}, f32[776,128]{1,0:T(8,128)S(1)}, u32[]{:S(2)}, u32[]{:S(2)}) collective-permute-start(f32[776,128]{1,0:T(8,128)S(1)} %collective-permute-done.7.refs_9_.refs_10_.refs_4_.a4.refs_11_.b_ref), channel_id=1, source_target_pairs={{0,4},{4,0},{8,12},{12,8},{16,20},{20,16},{24,28},{28,24},{32,36},... | collective-permute-start | bytes 1191944 | tf_op jit(solution)/shard_map/turn4/ppermute | solution.py:593
  61.3 1.9 %collective-permute-start.9 = (f32[768,128]{1,0:T(8,128)S(1)}, f32[768,128]{1,0:T(8,128)S(1)}, u32[]{:S(2)}, u32[]{:S(2)}) collective-permute-start(f32[768,128]{1,0:T(8,128)S(1)} %get-tuple-element.91), channel_id=1, source_target_pairs={{0,4},{4,0},{8,12},{12,8},{16,20},{20,16},{24,28},{28,24},{32,36},... | collective-permute-start | bytes 1179656 | tf_op jit(solution)/shard_map/half4/ppermute | solution.py:593
  63.3 14.2 %collective-permute-start.13 = (f32[768,128]{1,0:T(8,128)S(1)}, f32[768,128]{1,0:T(8,128)S(1)}, u32[]{:S(2)}, u32[]{:S(2)}) collective-permute-start(f32[768,128]{1,0:T(8,128)S(1)} %get-tuple-element.121), channel_id=1, source_target_pairs={{0,96},{4,100},{8,104},{12,108},{16,112},{20,116},{24,120},{28,124... | collective-permute-start | bytes 1179656 | tf_op jit(solution)/shard_map/down4/ppermute | solution.py:593
  77.0 3.0 %collective-permute-start.10 = (f32[1024,128]{1,0:T(8,128)S(1)}, f32[1024,128]{1,0:T(8,128)S(1)}, u32[]{:S(2)}, u32[]{:S(2)}) collective-permute-start(f32[1024,128]{1,0:T(8,128)S(1)} %get-tuple-element.104), channel_id=1, source_target_pairs={{0,4},{4,0},{8,12},{12,8},{16,20},{20,16},{24,28},{28,24},{32,36},... | collective-permute-start | bytes 1572872 | tf_op jit(solution)/shard_map/share/ppermute | solution.py:593
  77.1 2.4 %collective-permute-start.14 = (f32[768,128]{1,0:T(8,128)S(1)}, f32[768,128]{1,0:T(8,128)S(1)}, u32[]{:S(2)}, u32[]{:S(2)}) collective-permute-start(f32[768,128]{1,0:T(8,128)S(1)} %get-tuple-element.124), channel_id=1, source_target_pairs={{0,4},{4,0},{8,12},{12,8},{16,20},{20,16},{24,28},{28,24},{32,36},... | collective-permute-start | bytes 1179656 | tf_op jit(solution)/shard_map/half3/ppermute | solution.py:593
  79.7 11.2 %collective-permute-start.15 = (f32[768,128]{1,0:T(8,128)S(1)}, f32[768,128]{1,0:T(8,128)S(1)}, u32[]{:S(2)}, u32[]{:S(2)}) collective-permute-start(f32[768,128]{1,0:T(8,128)S(1)} %get-tuple-element.126), channel_id=1, source_target_pairs={{0,32},{4,36},{8,40},{12,44},{16,48},{20,52},{24,56},{28,60},{32,0... | collective-permute-start | bytes 1179656 | tf_op jit(solution)/shard_map/down3/ppermute | solution.py:593
  79.8 11.1 %collective-permute-start.16 = (f32[768,128]{1,0:T(8,128)S(1)}, f32[768,128]{1,0:T(8,128)S(1)}, u32[]{:S(2)}, u32[]{:S(2)}) collective-permute-start(f32[768,128]{1,0:T(8,128)S(1)} %get-tuple-element.129), channel_id=1, source_target_pairs={{0,4},{4,0},{8,12},{12,8},{16,20},{20,16},{24,28},{28,24},{32,36},... | collective-permute-start | bytes 1179656 | tf_op jit(solution)/shard_map/half2/ppermute | solution.py:593
  80.0 10.1 %collective-permute-start.11 = (f32[512,128]{1,0:T(8,128)S(1)}, f32[512,128]{1,0:T(8,128)S(1)}, u32[]{:S(2)}, u32[]{:S(2)}) collective-permute-start(f32[512,128]{1,0:T(8,128)S(1)} %get-tuple-element.106), channel_id=1, source_target_pairs={{0,96},{4,100},{8,104},{12,108},{16,112},{20,116},{24,120},{28,124... | collective-permute-start | bytes 786440 | tf_op jit(solution)/shard_map/share_z2/ppermute | solution.py:593
  91.0 14.4 %collective-permute-start.17 = (f32[768,128]{1,0:T(8,128)S(1)}, f32[768,128]{1,0:T(8,128)S(1)}, u32[]{:S(2)}, u32[]{:S(2)}) collective-permute-start(f32[768,128]{1,0:T(8,128)S(1)} %get-tuple-element.131), channel_id=1, source_target_pairs={{0,24},{4,28},{8,16},{12,20},{16,8},{20,12},{24,0},{28,4},{32,56},... | collective-permute-start | bytes 1179656 | tf_op jit(solution)/shard_map/down2/ppermute | solution.py:593
  93.9 11.6 %collective-permute-start.19 = (f32[768,128]{1,0:T(8,128)S(1)}, f32[768,128]{1,0:T(8,128)S(1)}, u32[]{:S(2)}, u32[]{:S(2)}) collective-permute-start(f32[768,128]{1,0:T(8,128)S(1)} %get-tuple-element.136), channel_id=1, source_target_pairs={{0,4},{4,0},{8,12},{12,8},{16,20},{20,16},{24,28},{28,24},{32,36},... | collective-permute-start | bytes 1179656 | tf_op jit(solution)/shard_map/half1/ppermute | solution.py:593
  93.9 5.9 %collective-permute-start.12 = (f32[256,128]{1,0:T(8,128)S(1)}, f32[256,128]{1,0:T(8,128)S(1)}, u32[]{:S(2)}, u32[]{:S(2)}) collective-permute-start(f32[256,128]{1,0:T(8,128)S(1)} %get-tuple-element.112), channel_id=1, source_target_pairs={{0,32},{4,36},{8,40},{12,44},{16,48},{20,52},{24,56},{28,60},{32,0... | collective-permute-start | bytes 393224 | tf_op jit(solution)/shard_map/share_z1/ppermute | solution.py:593
  94.2 21.3 %collective-permute-start.23 = (f32[776,128]{1,0:T(8,128)S(1)}, f32[776,128]{1,0:T(8,128)S(1)}, u32[]{:S(2)}, u32[]{:S(2)}) collective-permute-start(f32[776,128]{1,0:T(8,128)S(1)} %join4.1.own_ref), channel_id=1, source_target_pairs={{0,4},{4,0},{8,12},{12,8},{16,20},{20,16},{24,28},{28,24},{32,36},... | collective-permute-start | bytes 1191944 | tf_op jit(solution)/shard_map/fin/ppermute | solution.py:593
  99.8 5.6 %collective-permute-start.18 = (f32[128,128]{1,0:T(8,128)S(1)}, f32[128,128]{1,0:T(8,128)S(1)}, u32[]{:S(2)}, u32[]{:S(2)}) collective-permute-start(f32[128,128]{1,0:T(8,128)S(1)} %get-tuple-element.132), channel_id=1, source_target_pairs={{0,8},{4,12},{8,0},{12,4},{16,24},{20,28},{24,16},{28,20},{32,40},... | collective-permute-start | bytes 196616 | tf_op jit(solution)/shard_map/share_x1/ppermute | solution.py:593
  105.6 13.7 %collective-permute-start.20 = (f32[768,128]{1,0:T(8,128)S(1)}, f32[768,128]{1,0:T(8,128)S(1)}, u32[]{:S(2)}, u32[]{:S(2)}) collective-permute-start(f32[768,128]{1,0:T(8,128)S(1)} %get-tuple-element.138), channel_id=1, source_target_pairs={{0,8},{4,12},{8,0},{12,4},{16,24},{20,28},{24,16},{28,20},{32,40},... | collective-permute-start | bytes 1179656 | tf_op jit(solution)/shard_map/down1/ppermute | solution.py:593
  107.7 17.6 %collective-permute-start.25 = (f32[1536,128]{1,0:T(8,128)S(1)}, f32[1536,128]{1,0:T(8,128)S(1)}, u32[]{:S(2)}, u32[]{:S(2)}) collective-permute-start(f32[1536,128]{1,0:T(8,128)S(1)} %get-tuple-element.94), channel_id=1, source_target_pairs={{4,0},{12,8},{20,16},{28,24},{36,32},{44,40},{52,48},{60,56},{68,6... | collective-permute-start | bytes 2359304 | tf_op jit(solution)/shard_map/ppermute | solution.py:658
  109.0 6.0 %collective-permute-start.21 = (f32[128,128]{1,0:T(8,128)S(1)}, f32[128,128]{1,0:T(8,128)S(1)}, u32[]{:S(2)}, u32[]{:S(2)}) collective-permute-start(f32[128,128]{1,0:T(8,128)S(1)} %row.1.refs_0_), channel_id=1, source_target_pairs={{0,3},{1,2},{2,1},{3,0},{4,7},{5,6},{6,5},{7,4},{8,11},{9,10},{10,... | collective-permute-start | bytes 196616 | tf_op jit(solution)/shard_map/share_y2/ppermute | solution.py:598
  115.0 4.3 %collective-permute-start.22 = (f32[128,128]{1,0:T(8,128)S(1)}, f32[128,128]{1,0:T(8,128)S(1)}, u32[]{:S(2)}, u32[]{:S(2)}) collective-permute-start(f32[128,128]{1,0:T(8,128)S(1)} %row2.1.a_ref), channel_id=1, source_target_pairs={{0,1},{1,0},{2,3},{3,2},{4,5},{5,4},{6,7},{7,6},{8,9},{9,8},{10,11... | collective-permute-start | bytes 196616 | tf_op jit(solution)/shard_map/share_y1/ppermute | solution.py:598
  119.4 5.9 %collective-permute-start.24 = (f32[768,128]{1,0:T(8,128)S(1)}, f32[768,128]{1,0:T(8,128)S(1)}, u32[]{:S(2)}, u32[]{:S(2)}) collective-permute-start(f32[768,128]{1,0:T(8,128)S(1)} %w_chip.1.wa), channel_id=1, source_target_pairs={{0,4},{4,0},{8,12},{12,8},{16,20},{20,16},{24,28},{28,24},{32,36},... | collective-permute-start | bytes 1179656 | tf_op jit(solution)/shard_map/half0/ppermute | solution.py:593
  119.5 5.2 %collective-permute-start.26 = (f32[64,128]{1,0:T(8,128)S(1)}, f32[64,128]{1,0:T(8,128)S(1)}, u32[]{:S(2)}, u32[]{:S(2)}) collective-permute-start(f32[64,128]{1,0:T(8,128)S(1)} %get-tuple-element.145), channel_id=1, source_target_pairs={{0,24},{4,28},{8,16},{12,20},{16,8},{20,12},{24,0},{28,4},{32,56},... | collective-permute-start | bytes 98312 | tf_op jit(solution)/shard_map/share_x2/ppermute | solution.py:593
  (5 other events, 14.3 us)
